TPU v7x, 32 devices: a whole 2x2x4 slice. The times are simulated.
32 devices in a mesh: dp: 8 (over y, x, core), tensor: 4 (over z).
Axes of the slice: x: 2, y: 2, z: 4, core: 2. Of those that a mesh axis runs over, the one named last changes fastest.
Arguments:
- states_in: bfloat16 [8192, 1152], P(('dp', 'tensor')), may hold values from -6 to 6
- teacher: bfloat16 [8192, 1152], P(('dp', 'tensor')), may hold values from -6 to 6
- valid_counts: int32 [16], P('dp'), may hold values from 128 to 512
- attn_norm_gain: bfloat16 [1152], replicated, may hold values from 0.25 to 1.75
- attn_norm_bias: bfloat16 [1152], replicated, may hold values from -0.1875 to 0.1875
- query_weight: bfloat16 [1152, 1152], P(None, 'tensor'), may hold values from -0.1875 to 0.1875
- query_bias: bfloat16 [1152], P('tensor'), may hold values from -3 to 3
- key_weight: bfloat16 [1152, 1152], P(None, 'tensor'), may hold values from -0.1875 to 0.1875
- value_weight: bfloat16 [1152, 1152], P(None, 'tensor'), may hold values from -0.1875 to 0.1875
- value_bias: bfloat16 [1152], P('tensor'), may hold values from -0.1875 to 0.1875
- output_weight: bfloat16 [1152, 1152], P('tensor'), may hold values from -3 to 3
- output_bias: bfloat16 [1152], replicated, may hold values from -0.625 to 0.625
- mlp_norm_gain: bfloat16 [1152], replicated, may hold values from 0.25 to 1.75
- mlp_norm_bias: bfloat16 [1152], replicated, may hold values from -0.625 to 0.625
- up_weight: bfloat16 [1152, 4304], P(None, 'tensor'), may hold values from -0.1875 to 0.1875
- up_bias: bfloat16 [4304], P('tensor'), may hold values from -1.25 to 1.25
- down_weight: bfloat16 [4304, 1152], P('tensor'), may hold values from -0.09375 to 0.09375
- down_bias: bfloat16 [1152], replicated, may hold values from -0.625 to 0.625
Outputs:
- out_states: bfloat16 [8192, 1152], P(('dp', 'tensor'))
- distill_loss: float32 [], replicated
- grad_input: bfloat16 [8192, 1152], P(('dp', 'tensor'))
- grad_attn_norm_gain: float32 [1152], replicated
- grad_attn_norm_bias: float32 [1152], replicated
- grad_query_weight: float32 [1152, 1152], P(None, 'tensor')
- grad_query_bias: float32 [1152], P('tensor')
- grad_key_weight: float32 [1152, 1152], P(None, 'tensor')
- grad_value_weight: float32 [1152, 1152], P(None, 'tensor')
- grad_value_bias: float32 [1152], P('tensor')
- grad_output_weight: float32 [1152, 1152], P('tensor')
- grad_output_bias: float32 [1152], replicated
- grad_mlp_norm_gain: float32 [1152], replicated
- grad_mlp_norm_bias: float32 [1152], replicated
- grad_up_weight: float32 [1152, 4304], P(None, 'tensor')
- grad_up_bias: float32 [4304], P('tensor')
- grad_down_weight: float32 [4304, 1152], P('tensor')
- grad_down_bias: float32 [1152], replicated
Inputs may be any that keep to these rules, and one draw needn't show every extreme that they name: `valid_counts`: the valid patches of an image are its first count patch slots.
All inputs are finite; a program needn't handle non-finite values.
Results may differ from a plain program's by a relative error of at most 0.012.
The roundings to bfloat16 on the way count: a program that leaves them out, or rounds other values in their place, can miss the bound.
Values may be sent and summed in bfloat16 or wider, within the bound.
No kernel may reach another device: no remote copies, remote signals or barrier semaphores. Data moves between devices by JAX's collectives and lax.ppermute only.
A program may use at most 128 MiB of HBM per device.

v0:
```python
import math

import jax
import jax.numpy as jnp
from jax import lax
from jax.sharding import PartitionSpec as P

HEAD_DIM = 72


def layer_norm(values, gain, bias):
    centre = jnp.mean(values, axis=-1, keepdims=True)
    shifted = values - centre
    spread = jnp.mean(shifted * shifted, axis=-1, keepdims=True)
    return shifted * lax.rsqrt(spread + 1e-06) * gain + bias


def gelu_tanh(values):
    return jax.nn.gelu(values, approximate=True)


def times_transpose(left, right):
    return lax.dot_general(
        left, right, (((1,), (1,)), ((), ())), preferred_element_type=jnp.float32
    )


def transpose_times(left, right):
    return lax.dot_general(
        left, right, (((0,), (0,)), ((), ())), preferred_element_type=jnp.float32
    )


def split_heads(block, image_index, seq_len):
    return block[image_index * seq_len : (image_index + 1) * seq_len].reshape(seq_len, -1, HEAD_DIM)


def masked_scores(query_view, key_view, count_valid, score_scale):
    scores = (
        jnp.einsum("qhd,khd->hqk", query_view, key_view, preferred_element_type=jnp.float32)
        * score_scale
    )
    key_alive = jnp.arange(key_view.shape[0], dtype=jnp.int32) < count_valid
    return jnp.where(key_alive[None, None, :], scores, -1e30)


def per_device(
    states_in,
    teacher,
    valid_counts,
    attn_norm_gain,
    attn_norm_bias,
    query_weight,
    query_bias,
    key_weight,
    value_weight,
    value_bias,
    output_weight,
    output_bias,
    mlp_norm_gain,
    mlp_norm_bias,
    up_weight,
    up_bias,
    down_weight,
    down_bias,
):
    row_count = states_in.shape[0]
    tensor_size = lax.axis_size("tensor")
    group_rows = row_count * tensor_size
    image_count = valid_counts.shape[0]
    seq_len = group_rows // image_count
    score_scale = 1.0 / math.sqrt(HEAD_DIM)
    local_index = lax.axis_index("tensor")
    row_ids = local_index * row_count + jnp.arange(row_count, dtype=jnp.int32)
    image_ids = row_ids // seq_len
    positions = row_ids % seq_len
    picks = image_ids[:, None] == jnp.arange(image_count, dtype=jnp.int32)[None, :]
    row_limits = jnp.sum(jnp.where(picks, valid_counts[None, :], 0), axis=1)
    row_valid = (positions < row_limits).astype(jnp.float32)
    count_here = jnp.sum(row_valid)
    gain_one = attn_norm_gain.astype(jnp.float32)
    bias_one = attn_norm_bias.astype(jnp.float32)
    gain_two = mlp_norm_gain.astype(jnp.float32)
    bias_two = mlp_norm_bias.astype(jnp.float32)
    states_f = states_in.astype(jnp.float32)
    ln_one, norm_one_back = jax.vjp(layer_norm, states_f, gain_one, bias_one)
    ln_one_all = lax.all_gather(ln_one.astype(jnp.bfloat16), "tensor", axis=0, tiled=True)
    query = (
        jnp.dot(ln_one_all, query_weight, preferred_element_type=jnp.float32)
        + query_bias.astype(jnp.float32)
    ).astype(jnp.bfloat16)
    keys = jnp.dot(ln_one_all, key_weight, preferred_element_type=jnp.float32).astype(jnp.bfloat16)
    values = (
        jnp.dot(ln_one_all, value_weight, preferred_element_type=jnp.float32)
        + value_bias.astype(jnp.float32)
    ).astype(jnp.bfloat16)
    context_list = []
    logsum_list = []
    for image_index in range(image_count):
        query_view = split_heads(query, image_index, seq_len)
        key_view = split_heads(keys, image_index, seq_len)
        value_view = split_heads(values, image_index, seq_len)
        scores = masked_scores(query_view, key_view, valid_counts[image_index], score_scale)
        top = jnp.max(scores, axis=-1, keepdims=True)
        exps = jnp.exp(scores - top)
        totals = jnp.sum(exps, axis=-1, keepdims=True)
        probs = exps / totals
        logsum_list.append(top + jnp.log(totals))
        mixed = jnp.einsum(
            "hqk,khd->qhd",
            probs.astype(jnp.bfloat16),
            value_view,
            preferred_element_type=jnp.float32,
        )
        context_list.append(mixed.reshape(seq_len, -1).astype(jnp.bfloat16))
    context = jnp.concatenate(context_list, axis=0)
    attn_out = lax.psum_scatter(
        jnp.dot(context, output_weight, preferred_element_type=jnp.float32),
        "tensor",
        scatter_dimension=0,
        tiled=True,
    )
    hidden_one = states_f + attn_out + output_bias.astype(jnp.float32)
    ln_two, norm_two_back = jax.vjp(layer_norm, hidden_one, gain_two, bias_two)
    ln_two_all = lax.all_gather(ln_two.astype(jnp.bfloat16), "tensor", axis=0, tiled=True)
    pre_act = jnp.dot(ln_two_all, up_weight, preferred_element_type=jnp.float32) + up_bias.astype(
        jnp.float32
    )
    activ_f, gelu_back = jax.vjp(gelu_tanh, pre_act)
    activ = activ_f.astype(jnp.bfloat16)
    mlp_out = lax.psum_scatter(
        jnp.dot(activ, down_weight, preferred_element_type=jnp.float32),
        "tensor",
        scatter_dimension=0,
        tiled=True,
    )
    hidden_two = hidden_one + mlp_out + down_bias.astype(jnp.float32)
    out_states = hidden_two.astype(jnp.bfloat16)
    error_rows = (hidden_two - teacher.astype(jnp.float32)) * row_valid[:, None]
    squares_here = jnp.sum(error_rows * error_rows)
    squares_total, token_total = lax.psum((squares_here, count_here), ("dp", "tensor"))
    distill_loss = squares_total / token_total
    grad_two = error_rows * (2.0 / token_total)
    cot_two = lax.all_gather(grad_two.astype(jnp.bfloat16), "tensor", axis=0, tiled=True)
    grad_down = transpose_times(activ, cot_two)
    grad_down_bias = jnp.sum(grad_two, axis=0)
    grad_activ = times_transpose(cot_two, down_weight)
    grad_pre = gelu_back(grad_activ)[0].astype(jnp.bfloat16)
    grad_up = transpose_times(ln_two_all, grad_pre)
    grad_up_bias = jnp.sum(grad_pre.astype(jnp.float32), axis=0)
    grad_ln_two = lax.psum_scatter(
        times_transpose(grad_pre, up_weight), "tensor", scatter_dimension=0, tiled=True
    )
    grad_hidden, grad_gain_two, grad_bias_two = norm_two_back(grad_ln_two)
    grad_one = grad_two + grad_hidden
    cot_one = lax.all_gather(grad_one.astype(jnp.bfloat16), "tensor", axis=0, tiled=True)
    grad_out = transpose_times(context, cot_one)
    grad_out_bias = jnp.sum(grad_one, axis=0)
    grad_context = times_transpose(cot_one, output_weight).astype(jnp.bfloat16)
    grad_query_list = []
    grad_key_list = []
    grad_value_list = []
    for image_index in range(image_count):
        query_view = split_heads(query, image_index, seq_len)
        key_view = split_heads(keys, image_index, seq_len)
        value_view = split_heads(values, image_index, seq_len)
        grad_view = split_heads(grad_context, image_index, seq_len)
        scores = masked_scores(query_view, key_view, valid_counts[image_index], score_scale)
        probs = jnp.exp(scores - logsum_list[image_index])
        grad_probs = jnp.einsum(
            "qhd,khd->hqk", grad_view, value_view, preferred_element_type=jnp.float32
        )
        grad_value_view = jnp.einsum(
            "hqk,qhd->khd",
            probs.astype(jnp.bfloat16),
            grad_view,
            preferred_element_type=jnp.float32,
        )
        inner = jnp.sum(grad_probs * probs, axis=-1, keepdims=True)
        grad_scores = (probs * (grad_probs - inner)).astype(jnp.bfloat16)
        grad_query_view = (
            jnp.einsum("hqk,khd->qhd", grad_scores, key_view, preferred_element_type=jnp.float32)
            * score_scale
        )
        grad_key_view = (
            jnp.einsum("hqk,qhd->khd", grad_scores, query_view, preferred_element_type=jnp.float32)
            * score_scale
        )
        grad_query_list.append(grad_query_view.reshape(seq_len, -1).astype(jnp.bfloat16))
        grad_key_list.append(grad_key_view.reshape(seq_len, -1).astype(jnp.bfloat16))
        grad_value_list.append(grad_value_view.reshape(seq_len, -1).astype(jnp.bfloat16))
    grad_query_all = jnp.concatenate(grad_query_list, axis=0)
    grad_key_all = jnp.concatenate(grad_key_list, axis=0)
    grad_value_all = jnp.concatenate(grad_value_list, axis=0)
    grad_query = transpose_times(ln_one_all, grad_query_all)
    grad_query_bias = jnp.sum(grad_query_all.astype(jnp.float32), axis=0)
    grad_key = transpose_times(ln_one_all, grad_key_all)
    grad_value = transpose_times(ln_one_all, grad_value_all)
    grad_value_bias = jnp.sum(grad_value_all.astype(jnp.float32), axis=0)
    grad_ln_one = lax.psum_scatter(
        times_transpose(grad_query_all, query_weight)
        + times_transpose(grad_key_all, key_weight)
        + times_transpose(grad_value_all, value_weight),
        "tensor",
        scatter_dimension=0,
        tiled=True,
    )
    grad_states, grad_gain_one, grad_bias_one = norm_one_back(grad_ln_one)
    grad_input = (grad_one + grad_states).astype(jnp.bfloat16)
    (
        grad_query,
        grad_query_bias,
        grad_key,
        grad_value,
        grad_value_bias,
        grad_out,
        grad_up,
        grad_up_bias,
        grad_down,
    ) = lax.psum(
        (
            grad_query,
            grad_query_bias,
            grad_key,
            grad_value,
            grad_value_bias,
            grad_out,
            grad_up,
            grad_up_bias,
            grad_down,
        ),
        "dp",
    )
    loss_member = jnp.zeros((), jnp.float32)
    summed = lax.psum(
        (
            grad_gain_one,
            grad_bias_one,
            grad_out_bias,
            grad_gain_two,
            grad_bias_two,
            grad_down_bias,
            loss_member,
        ),
        ("dp", "tensor"),
    )
    return (
        out_states,
        distill_loss,
        grad_input,
        summed[0],
        summed[1],
        grad_query,
        grad_query_bias,
        grad_key,
        grad_value,
        grad_value_bias,
        grad_out,
        summed[2],
        summed[3],
        summed[4],
        grad_up,
        grad_up_bias,
        grad_down,
        summed[5],
    )


def solution(mesh):
    placed = (
        P(("dp", "tensor"), None),
        P(("dp", "tensor"), None),
        P("dp"),
        P(),
        P(),
        P(None, "tensor"),
        P("tensor"),
        P(None, "tensor"),
        P(None, "tensor"),
        P("tensor"),
        P("tensor", None),
        P(),
        P(),
        P(),
        P(None, "tensor"),
        P("tensor"),
        P("tensor", None),
        P(),
    )
    return jax.shard_map(
        per_device,
        mesh=mesh,
        in_specs=placed,
        out_specs=(
            P(("dp", "tensor"), None),
            P(),
            P(("dp", "tensor"), None),
            P(),
            P(),
            P(None, "tensor"),
            P("tensor"),
            P(None, "tensor"),
            P(None, "tensor"),
            P("tensor"),
            P("tensor", None),
            P(),
            P(),
            P(),
            P(None, "tensor"),
            P("tensor"),
            P("tensor", None),
            P(),
        ),
        check_vma=False,
    )
```

profile of v0, /device:TPU:0, one launch (start us, length us, event | category | flops | bytes accessed | tf_op | source)
XLA Modules:
  0.0 862.6 jit_solution(6405624461404678379)
XLA Ops:
  11.4 2.2 fusion.40
  15.6 50.9 %all-gather.5.cloned.1.call-done = bf16[1024,1152]{1,0:T(8,128)(2,1)} async-done(((bf16[256,1152]{1,0:T(8,128)(2,1)}), bf16[1024,1152]{1,0:T(8,128)(2,1)}) %all-gather.5.cloned.1.call-update) | async-done | bytes 2359312 | tf_op jit(solution)/shard_map/all_gather | solution.py:87
  66.5 2.9 fusion.26
  78.1 3.7 fusion.48
  82.6 83.5 %reduce-scatter.5.cloned.1.call-done = f32[256,1152]{1,0:T(8,128)} async-done(((f32[1024,1152]{1,0:T(8,128)}), f32[256,1152]{1,0:T(8,128)}) %reduce-scatter.5.cloned.1.call-update) | async-done | bytes 1179664 | tf_op jit(solution)/shard_map/reduce_scatter | solution.py:117
  170.0 50.4 %all-gather.7.cloned.1.call-done = bf16[1024,1152]{1,0:T(8,128)(2,1)} async-done(((bf16[256,1152]{1,0:T(8,128)(2,1)}), bf16[1024,1152]{1,0:T(8,128)(2,1)}) %all-gather.7.cloned.1.call-update) | async-done | bytes 2359312 | tf_op jit(solution)/shard_map/all_gather | solution.py:125
  220.4 5.5 convolution_add_fusion.2
  225.9 2.1 copy-done.60
  228.0 5.4 fusion.66
  234.2 43.1 %psum.120 = f32[]{:T(128)} all-reduce(f32[]{:T(128)} %get-tuple-element.51), channel_id=1, replica_groups=mesh['dp'=8,'tensor'=4] {'dp','tensor'}, use_global_device_ids=true, to_apply=%region_14.15 | all-reduce | flops 1 | bytes 8 | tf_op jit(solution)/shard_map/psum | solution.py:141
  278.0 40.7 %reduce-scatter.7.cloned.1.call-done = f32[256,1152]{1,0:T(8,128)} async-done(((f32[1024,1152]{1,0:T(8,128)}), f32[256,1152]{1,0:T(8,128)}) %reduce-scatter.7.cloned.1.call-update) | async-done | bytes 1179664 | tf_op jit(solution)/shard_map/reduce_scatter | solution.py:131
  318.7 3.5 multiply_convert_fusion.3
  322.2 50.6 %all-gather.9.cloned.1.call-done = bf16[1024,1152]{1,0:T(8,128)(2,1)} async-done(((bf16[256,1152]{1,0:T(8,128)(2,1)}), bf16[1024,1152]{1,0:T(8,128)(2,1)}) %all-gather.9.cloned.1.call-update) | async-done | bytes 2359312 | tf_op jit(solution)/shard_map/all_gather | solution.py:144
  372.8 8.4 convert_reduce_fusion
  382.6 5.2 fusion.81
  387.9 84.2 %reduce-scatter.9.cloned.1.call-done = f32[256,1152]{1,0:T(8,128)} async-done(((f32[1024,1152]{1,0:T(8,128)}), f32[256,1152]{1,0:T(8,128)}) %reduce-scatter.9.cloned.1.call-update) | async-done | bytes 1179664 | tf_op jit(solution)/shard_map/reduce_scatter | solution.py:151
  477.3 50.4 %all-gather.11.cloned.1.call-done = bf16[1024,1152]{1,0:T(8,128)(2,1)} async-done(((bf16[256,1152]{1,0:T(8,128)(2,1)}), bf16[1024,1152]{1,0:T(8,128)(2,1)}) %all-gather.11.cloned.1.call-update) | async-done | bytes 2359312 | tf_op jit(solution)/shard_map/all_gather | solution.py:156
  527.6 2.8 convolution_convert_fusion
  543.8 3.7 convolution_add_fusion
  547.9 7.8 fusion.82
  555.7 8.6 fusion.65
  564.3 2.0 fusion.47
  566.3 2.0 fusion.49
  568.3 2.0 fusion.46
  570.3 2.0 fusion.50
  572.7 25.0 %all-reduce.1 = (f32[288]{0:T(512)}, f32[288]{0:T(512)}, f32[1076]{0:T(1024)}) all-reduce(f32[288]{0:T(512)S(1)} %convert_reduce_fusion.3, f32[288]{0:T(512)S(1)} %convert_reduce_fusion.2, f32[1076]{0:T(1024)S(1)} %get-tuple-element.43), channel_id=1, replica_groups=mesh['dp'=8,'tensor'=4] {'dp'}, use_global_device_ids=true, to_apply=%region_29.30 | all-reduce | flops 1652 | bytes 13216 | tf_op jit(solution)/shard_map/psum | solution.py:220
  597.7 34.0 %reduce-scatter.11.cloned.1.call-done = f32[256,1152]{1,0:T(8,128)} async-done(((f32[1024,1152]{1,0:T(8,128)}), f32[256,1152]{1,0:T(8,128)}) %reduce-scatter.11.cloned.1.call-update) | async-done | bytes 1179664 | tf_op jit(solution)/shard_map/reduce_scatter | solution.py:200
  634.1 43.0 %all-reduce = (f32[]{:T(128)}, f32[1152]{0:T(1024)}, f32[1152]{0:T(1024)}, f32[1152]{0:T(1024)}, f32[1152]{0:T(1024)}, /*index=5*/f32[1152]{0:T(1024)}, f32[1152]{0:T(1024)}) all-reduce(f32[]{:T(128)} %get-tuple-element.56, f32[1152]{0:T(1024)S(1)} %get-tuple-element.20, ...), channel_id=1, replica_groups=mesh['dp'=8,'tensor'=4] {'dp','tensor'}, use_global_device_ids=true, to_apply=%region_12.13 | all-reduce | flops 6913 | bytes 55304 | tf_op jit(solution)/shard_map/psum | solution.py:141
  679.7 161.9 %all-reduce.5.cloned.1.call-done = (f32[1152,288]{0,1:T(8,128)}, f32[1152,288]{0,1:T(8,128)}, f32[1152,288]{0,1:T(8,128)}, f32[288,1152]{1,0:T(8,128)}, f32[1152,1076]{0,1:T(8,128)}, /*index=5*/f32[1076,1152]{1,0:T(8,128)}) async-done(((f32[1152,288]{0,1:T(8,128)}, f32[1152,288]{0,1:T(8,128)}, f32[1152,288]{0,1:T(8,128)}, f32[288,1152]{1,0:T(8,128)}, f32[1152,1076]{0,1:T(8,128)}, ...) | async-done | bytes 15224848 | tf_op jit(solution)/shard_map/psum | solution.py:220
  841.6 2.6 copy.66
  848.7 2.3 copy.70
  851.0 2.5 copy.71
  (212 shorter events, 49.6 us)
Async XLA Ops:
  7.2 220.8 %copy-start = (bf16[1076,1152]{1,0:T(8,128)(2,1)S(1)}, bf16[1076,1152]{1,0:T(8,128)(2,1)}, u32[]{:S(2)}) copy-start(bf16[1076,1152]{1,0:T(8,128)(2,1)} %param.34) | copy-start | bytes 7437316
  7.2 6.5 copy-start.53
  7.2 6.5 copy-start.54
  7.2 6.5 copy-start.47
  7.2 59.2 %all-gather.5.cloned.1.call-start = ((), (), s32[]{:S(2)}) async-start(), calls=%async_computation.4 | async-start | bytes 2949120 | tf_op jit(solution)/shard_map/all_gather | solution.py:87
  13.6 152.5 %reduce-scatter.5.cloned.1.call-start = ((), (), s32[]{:S(2)}) async-start(), calls=%async_computation.5 | async-start | bytes 5898240 | tf_op jit(solution)/shard_map/reduce_scatter | solution.py:117
  70.7 5.9 copy-start.30
  77.9 3.9 copy-start.45
  81.9 84.2 %copy-start.8 = (bf16[256,1152]{1,0:T(8,128)(2,1)S(1)}, bf16[256,1152]{1,0:T(8,128)(2,1)}, u32[]{:S(2)}) copy-start(bf16[256,1152]{1,0:T(8,128)(2,1)} %param.18) | copy-start | bytes 1769476
  81.9 138.5 %all-gather.7.cloned.1.call-start = ((), (), s32[]{:S(2)}) async-start(), calls=%async_computation.6 | async-start | bytes 2949120 | tf_op jit(solution)/shard_map/all_gather | solution.py:125
  169.7 148.9 %reduce-scatter.7.cloned.1.call-start = ((), (), s32[]{:S(2)}) async-start(), calls=%async_computation.7 | async-start | bytes 5898240 | tf_op jit(solution)/shard_map/reduce_scatter | solution.py:131
  233.4 43.9 %copy-start.52 = (bf16[1152]{0:T(1024)(128)(2,1)S(1)}, bf16[1152]{0:T(1024)(128)(2,1)}, u32[]{:S(2)}) copy-start(bf16[1152]{0:T(1024)(128)(2,1)} %param.35) | copy-start | bytes 6916
  233.4 139.4 %all-gather.9.cloned.1.call-start = ((), (), s32[]{:S(2)}) async-start(), calls=%async_computation.8 | async-start | bytes 2949120 | tf_op jit(solution)/shard_map/all_gather | solution.py:144
  322.2 149.8 %reduce-scatter.9.cloned.1.call-start = ((), (), s32[]{:S(2)}) async-start(), calls=%async_computation.9 | async-start | bytes 5898240 | tf_op jit(solution)/shard_map/reduce_scatter | solution.py:151
  372.8 9.8 %copy-start.55 = (bf16[1152,1076]{0,1:T(8,128)(2,1)S(1)}, bf16[1152,1076]{0,1:T(8,128)(2,1)}, u32[]{:S(2)}) copy-start(bf16[1152,1076]{0,1:T(8,128)(2,1)} %param.32) | copy-start | bytes 7437316
  387.8 84.2 %copy-start.7 = (f32[256,1152]{1,0:T(8,128)S(1)}, f32[256,1152]{1,0:T(8,128)}, u32[]{:S(2)}) copy-start(f32[256,1152]{1,0:T(8,128)} %copy-done.6) | copy-start | bytes 3538948
  387.8 139.8 %all-gather.11.cloned.1.call-start = ((), (), s32[]{:S(2)}) async-start(), calls=%async_computation.10 | async-start | bytes 2949120 | tf_op jit(solution)/shard_map/all_gather | solution.py:156
  476.1 54.4 %copy-start.9 = (f32[256,1152]{1,0:T(8,128)}, f32[256,1152]{1,0:T(8,128)S(1)}, u32[]{:S(2)}) copy-start(f32[256,1152]{1,0:T(8,128)S(1)} %get-tuple-element.46) | copy-start | bytes 3538948
  476.1 51.6 %copy-start.37 = (bf16[288,1152]{1,0:T(8,128)(2,1)S(1)}, bf16[288,1152]{1,0:T(8,128)(2,1)}, u32[]{:S(2)}) copy-start(bf16[288,1152]{1,0:T(8,128)(2,1)} %param.28) | copy-start | bytes 1990660
  477.0 154.8 %reduce-scatter.11.cloned.1.call-start = ((), (), s32[]{:S(2)}) async-start(), calls=%async_computation.11 | async-start | bytes 5898240 | tf_op jit(solution)/shard_map/reduce_scatter | solution.py:200
  534.4 7.8 copy-start.32
  534.9 5.7 copy-start.15
  547.5 294.0 %all-reduce.5.cloned.1.call-start = ((), (), s32[]{:S(2)}) async-start(), calls=%async_computation.12 | async-start | bytes 30523392 | tf_op jit(solution)/shard_map/psum | solution.py:220
  547.8 7.8 copy-start.58
  555.6 8.6 copy-start.44
  555.6 8.6 copy-start.46
  555.6 8.6 copy-start.59
  572.3 106.1 %copy-start.10 = (f32[256,1152]{1,0:T(8,128)S(1)}, f32[256,1152]{1,0:T(8,128)}, u32[]{:S(2)}) copy-start(f32[256,1152]{1,0:T(8,128)} %copy-done.9) | copy-start | bytes 3538948
  841.6 3.7 copy-start.26
  845.3 3.5 copy-start.12
  846.3 4.7 slice-start
  851.0 3.5 copy-start.1
  (41 other events, 75.5 us)
Sparse Core Ops, SparseCore 0:
  13.7 52.6 all-gather.4
  82.0 84.0 reduce-scatter.4
  169.9 50.4 all-gather.6
  233.5 85.0 reduce-scatter.6
  322.3 50.4 all-gather.8
  387.9 84.0 reduce-scatter.8
  477.1 50.4 all-gather.10
  547.7 84.0 reduce-scatter.10
  638.2 203.3 all-reduce.4
where the time goes:
time: 871 us; the launch traced here: 863 us
  waiting for transfers between devices  607 us (70%)
  blocking collectives  111 us (13%)
  matrix products  76.7 us (9%)
  other arithmetic  26.3 us (3%)
  local copies, waits for them, and re-layouts  22.6 us (3%)
  between operations  18.2 us (2%)
    psum x1, waiting for transfers between devices, per_device(): lax.psum((grad_query, grad_query_bias, grad_key, grad_value, grad_value_b...  162 us
    psum x2, blocking collectives, per_device(): lax.psum((squares_here, count_here), ('dp', 'tensor'))  86.1 us
    reduce_scatter x1, waiting for transfers between devices, per_device(): lax.psum_scatter(times_transpose(grad_pre, up_weight), 'tensor', scatter_...  84.2 us
    reduce_scatter x1, waiting for transfers between devices, per_device(): lax.psum_scatter(jnp.dot(context, output_weight, preferred_element_type=j...  83.5 us
    all_gather x1, waiting for transfers between devices, per_device(): lax.all_gather(ln_one.astype(jnp.bfloat16), 'tensor', axis=0, tiled=True)  50.9 us
    all_gather x1, waiting for transfers between devices, per_device(): lax.all_gather(grad_two.astype(jnp.bfloat16), 'tensor', axis=0, tiled=True)  50.6 us
    all_gather x1, waiting for transfers between devices, per_device(): lax.all_gather(ln_two.astype(jnp.bfloat16), 'tensor', axis=0, tiled=True)  50.4 us
    all_gather x1, waiting for transfers between devices, per_device(): lax.all_gather(grad_one.astype(jnp.bfloat16), 'tensor', axis=0, tiled=True)  50.4 us
  transfers between devices with their start and end apart: 9, of which 9 were waited for; matrix products, arithmetic and copies ran while one was open for 4% of the time, Pallas kernels for 0%

commit v1 on v0

v1 whole, which is shorter than its diff:
```python
import math

import jax
import jax.numpy as jnp
from jax import lax
from jax.sharding import PartitionSpec as P

HEAD_DIM = 72


def layer_norm(values, gain, bias):
    centre = jnp.mean(values, axis=-1, keepdims=True)
    shifted = values - centre
    spread = jnp.mean(shifted * shifted, axis=-1, keepdims=True)
    return shifted * lax.rsqrt(spread + 1e-06) * gain + bias


def gelu_tanh(values):
    return jax.nn.gelu(values, approximate=True)


def times_transpose(left, right):
    return lax.dot_general(
        left, right, (((1,), (1,)), ((), ())), preferred_element_type=jnp.float32
    )


def transpose_times(left, right):
    return lax.dot_general(
        left, right, (((0,), (0,)), ((), ())), preferred_element_type=jnp.float32
    )


def exchange(value, axis, flip):
    size = lax.axis_size(axis)
    return lax.ppermute(value, axis, [(index, index ^ flip) for index in range(size)])


def gather_parts(value, axis):
    return [value] + [exchange(value, axis, flip) for flip in range(1, lax.axis_size(axis))]


def scatter_sum(parts, axis):
    total = parts[0]
    for flip in range(len(parts) - 1, 0, -1):
        total = total + exchange(parts[flip].astype(jnp.bfloat16), axis, flip).astype(jnp.float32)
    return total


def butterfly(value, axis):
    flip = 1
    while flip < lax.axis_size(axis):
        value = value + exchange(value, axis, flip)
        flip *= 2
    return value


def split_heads(block):
    return block.reshape(block.shape[0], -1, HEAD_DIM)


def masked_scores(query_view, key_view, key_alive, score_scale):
    scores = (
        jnp.einsum("qhd,khd->hqk", query_view, key_view, preferred_element_type=jnp.float32)
        * score_scale
    )
    return jnp.where(key_alive[None, None, :], scores, -1e30)


def per_device(
    states_in,
    teacher,
    valid_counts,
    attn_norm_gain,
    attn_norm_bias,
    query_weight,
    query_bias,
    key_weight,
    value_weight,
    value_bias,
    output_weight,
    output_bias,
    mlp_norm_gain,
    mlp_norm_bias,
    up_weight,
    up_bias,
    down_weight,
    down_bias,
):
    f32, bf16 = jnp.float32, jnp.bfloat16
    rows = states_in.shape[0]
    tensor_size = lax.axis_size("tensor")
    image_count = valid_counts.shape[0]
    seq_len = rows * tensor_size // image_count
    share = seq_len // rows
    score_scale = 1.0 / math.sqrt(HEAD_DIM)
    here = lax.axis_index("tensor")
    image_base = here // share
    limits = []
    for image_index in range(image_count):
        picks = jnp.arange(image_count, dtype=jnp.int32) == (image_base ^ image_index)
        limits.append(jnp.sum(jnp.where(picks, valid_counts, 0)))
    alive = []
    for image_index in range(image_count):
        places = [
            ((here ^ flip) % share) * rows + jnp.arange(rows, dtype=jnp.int32)
            for flip in range(share)
        ]
        alive.append(jnp.concatenate(places) < limits[image_index])
    row_valid = alive[0][:rows].astype(f32)
    token_total = butterfly(jnp.sum(valid_counts).reshape(1, 1), "dp").astype(f32)[0, 0]
    gain_one = attn_norm_gain.astype(f32)
    bias_one = attn_norm_bias.astype(f32)
    gain_two = mlp_norm_gain.astype(f32)
    bias_two = mlp_norm_bias.astype(f32)
    states_f = states_in.astype(f32)
    ln_one, norm_one_back = jax.vjp(layer_norm, states_f, gain_one, bias_one)
    ln_one_parts = gather_parts(ln_one.astype(bf16), "tensor")
    ln_one_img = [
        jnp.concatenate(ln_one_parts[i * share : (i + 1) * share], axis=0)
        for i in range(image_count)
    ]
    saved = []
    context_list = []
    for i in range(image_count):
        query = (
            jnp.dot(ln_one_img[i], query_weight, preferred_element_type=f32)
            + query_bias.astype(f32)
        ).astype(bf16)
        keys = jnp.dot(ln_one_img[i], key_weight, preferred_element_type=f32).astype(bf16)
        values = (
            jnp.dot(ln_one_img[i], value_weight, preferred_element_type=f32)
            + value_bias.astype(f32)
        ).astype(bf16)
        query_view, key_view, value_view = split_heads(query), split_heads(keys), split_heads(values)
        scores = masked_scores(query_view, key_view, alive[i], score_scale)
        top = jnp.max(scores, axis=-1, keepdims=True)
        exps = jnp.exp(scores - top)
        totals = jnp.sum(exps, axis=-1, keepdims=True)
        probs = exps / totals
        mixed = jnp.einsum(
            "hqk,khd->qhd", probs.astype(bf16), value_view, preferred_element_type=f32
        )
        context_list.append(mixed.reshape(seq_len, -1).astype(bf16))
        saved.append((query_view, key_view, value_view, top + jnp.log(totals)))
    attn_parts = []
    for i in range(image_count):
        partial = jnp.dot(context_list[i], output_weight, preferred_element_type=f32)
        attn_parts += [partial[s * rows : (s + 1) * rows] for s in range(share)]
    attn_out = scatter_sum(attn_parts, "tensor")
    hidden_one = states_f + attn_out + output_bias.astype(f32)
    ln_two, norm_two_back = jax.vjp(layer_norm, hidden_one, gain_two, bias_two)
    ln_two_all = jnp.concatenate(gather_parts(ln_two.astype(bf16), "tensor"), axis=0)
    pre_act = jnp.dot(ln_two_all, up_weight, preferred_element_type=f32) + up_bias.astype(f32)
    activ_f, gelu_back = jax.vjp(gelu_tanh, pre_act)
    activ = activ_f.astype(bf16)
    mlp_partial = jnp.dot(activ, down_weight, preferred_element_type=f32)
    mlp_out = scatter_sum(
        [mlp_partial[s * rows : (s + 1) * rows] for s in range(tensor_size)], "tensor"
    )
    hidden_two = hidden_one + mlp_out + down_bias.astype(f32)
    out_states = hidden_two.astype(bf16)
    error_rows = (hidden_two - teacher.astype(f32)) * row_valid[:, None]
    squares_here = jnp.sum(error_rows * error_rows)
    grad_two = error_rows * (2.0 / token_total)
    cot_two = jnp.concatenate(gather_parts(grad_two.astype(bf16), "tensor"), axis=0)
    grad_down = transpose_times(activ, cot_two)
    grad_down_bias = jnp.sum(grad_two, axis=0)
    grad_activ = times_transpose(cot_two, down_weight)
    grad_pre = gelu_back(grad_activ)[0].astype(bf16)
    grad_up = transpose_times(grad_pre, ln_two_all)
    grad_up_bias = jnp.sum(grad_pre.astype(f32), axis=0)
    gln_partial = times_transpose(grad_pre, up_weight)
    grad_ln_two = scatter_sum(
        [gln_partial[s * rows : (s + 1) * rows] for s in range(tensor_size)], "tensor"
    )
    mlp_grads = lax.psum((grad_down.astype(bf16), grad_up.astype(bf16)), "dp")
    grad_hidden, grad_gain_two, grad_bias_two = norm_two_back(grad_ln_two)
    grad_one = grad_two + grad_hidden
    cot_parts = gather_parts(grad_one.astype(bf16), "tensor")
    grad_out_bias = jnp.sum(grad_one, axis=0)
    grad_qkv = [[], [], []]
    cot_img = [
        jnp.concatenate(cot_parts[i * share : (i + 1) * share], axis=0)
        for i in range(image_count)
    ]
    for i in range(image_count):
        query_view, key_view, value_view, logsum = saved[i]
        grad_view = split_heads(times_transpose(cot_img[i], output_weight).astype(bf16))
        scores = masked_scores(query_view, key_view, alive[i], score_scale)
        probs = jnp.exp(scores - logsum)
        grad_probs = jnp.einsum("qhd,khd->hqk", grad_view, value_view, preferred_element_type=f32)
        grad_value_view = jnp.einsum(
            "hqk,qhd->khd", probs.astype(bf16), grad_view, preferred_element_type=f32
        )
        inner = jnp.sum(grad_probs * probs, axis=-1, keepdims=True)
        grad_scores = (probs * (grad_probs - inner)).astype(bf16)
        grad_query_view = (
            jnp.einsum("hqk,khd->qhd", grad_scores, key_view, preferred_element_type=f32)
            * score_scale
        )
        grad_key_view = (
            jnp.einsum("hqk,qhd->khd", grad_scores, query_view, preferred_element_type=f32)
            * score_scale
        )
        for slot, piece in enumerate((grad_query_view, grad_key_view, grad_value_view)):
            grad_qkv[slot].append(piece.reshape(seq_len, -1).astype(bf16))
    back_parts = []
    for i in range(image_count):
        partial = (
            times_transpose(grad_qkv[0][i], query_weight)
            + times_transpose(grad_qkv[1][i], key_weight)
            + times_transpose(grad_qkv[2][i], value_weight)
        )
        back_parts += [partial[s * rows : (s + 1) * rows] for s in range(share)]
    grad_ln_one = scatter_sum(back_parts, "tensor")
    context = jnp.concatenate(context_list, axis=0)
    cot_one = jnp.concatenate(cot_img, axis=0)
    ln_one_all = jnp.concatenate(ln_one_img, axis=0)
    grad_query_all, grad_key_all, grad_value_all = (jnp.concatenate(p, axis=0) for p in grad_qkv)
    grad_out = transpose_times(context, cot_one)
    grad_query = transpose_times(grad_query_all, ln_one_all)
    grad_key = transpose_times(grad_key_all, ln_one_all)
    grad_value = transpose_times(grad_value_all, ln_one_all)
    attn_grads = lax.psum(
        tuple(g.astype(bf16) for g in (grad_query, grad_key, grad_value, grad_out)), "dp"
    )
    grad_states, grad_gain_one, grad_bias_one = norm_one_back(grad_ln_one)
    grad_input = (grad_one + grad_states).astype(bf16)
    by_unit = lax.psum(
        (
            jnp.sum(grad_query_all.astype(f32), axis=0),
            jnp.sum(grad_value_all.astype(f32), axis=0),
            grad_up_bias,
        ),
        "dp",
    )
    summed = lax.psum(
        (
            grad_gain_one,
            grad_bias_one,
            grad_out_bias,
            grad_gain_two,
            grad_bias_two,
            grad_down_bias,
            squares_here,
        ),
        ("dp", "tensor"),
    )
    return (
        out_states,
        summed[6] / token_total,
        grad_input,
        summed[0],
        summed[1],
        attn_grads[0].T.astype(f32),
        by_unit[0],
        attn_grads[1].T.astype(f32),
        attn_grads[2].T.astype(f32),
        by_unit[1],
        attn_grads[3].astype(f32),
        summed[2],
        summed[3],
        summed[4],
        mlp_grads[1].T.astype(f32),
        by_unit[2],
        mlp_grads[0].astype(f32),
        summed[5],
    )


def solution(mesh):
    placed = (
        P(("dp", "tensor"), None),
        P(("dp", "tensor"), None),
        P("dp"),
        P(),
        P(),
        P(None, "tensor"),
        P("tensor"),
        P(None, "tensor"),
        P(None, "tensor"),
        P("tensor"),
        P("tensor", None),
        P(),
        P(),
        P(),
        P(None, "tensor"),
        P("tensor"),
        P("tensor", None),
        P(),
    )
    return jax.shard_map(
        per_device,
        mesh=mesh,
        in_specs=placed,
        out_specs=(
            P(("dp", "tensor"), None),
            P(),
            P(("dp", "tensor"), None),
            P(),
            P(),
            P(None, "tensor"),
            P("tensor"),
            P(None, "tensor"),
            P(None, "tensor"),
            P("tensor"),
            P("tensor", None),
            P(),
            P(),
            P(),
            P(None, "tensor"),
            P("tensor"),
            P("tensor", None),
            P(),
        ),
        check_vma=False,
    )
```

time: 871 us -> 584 us (0.67)
  waiting for transfers between devices: 607 us -> 321 us
  starting transfers between devices: 1.01 us -> 47.6 us
  blocking collectives: 111 us -> 65.2 us
  local copies, waits for them, and re-layouts: 22.6 us -> 10.5 us
    ppermute x0 -> x27, waiting for transfers between devices: none -> 306 us  [exchange(): lax.ppermute(value, axis, [(index, index ^ flip) for index in range(size)])]
    reduce_scatter x4 -> x0, waiting for transfers between devices: 242 us -> none  [the longest x1 84.2 us: per_device(): lax.psum_scatter(times_transpose(grad_pre, up_weight), 'tensor', scatter_...]
    all_gather x4 -> x0, waiting for transfers between devices: 202 us -> none  [the longest x1 50.9 us: per_device(): lax.all_gather(ln_one.astype(jnp.bfloat16), 'tensor', axis=0, tiled=True)]
    psum x1, waiting for transfers between devices: 162 us -> 15.4 us  [per_device(): lax.psum(tuple((g.astype(bf16) for g in (grad_query, grad_key, grad_value...]
    ppermute x0 -> x27, starting transfers between devices: none -> 47.5 us  [exchange(): lax.ppermute(value, axis, [(index, index ^ flip) for index in range(size)])]
    psum x3 -> x2, blocking collectives: 111 us -> 65.2 us  [the longest x1 40.5 us: per_device(): lax.psum((grad_gain_one, grad_bias_one, grad_out_bias, grad_gain_two, gra...]
    unnamed x134 -> x147, local copies, waits for them, and re-layouts: 21.9 us -> 5.97 us
    dot_general x10 -> x14, matrix products: 22.7 us -> 34.6 us  [the longest x1 16.1 us: per_device(): jnp.dot(ln_two_all, up_weight, preferred_element_type=f32)]
  transfers between devices with their start and end apart: 9 -> 28, of which waited for: 9 -> 20; matrix products, arithmetic and copies ran while one was open for 4% -> 8% of each run, Pallas kernels for 0% -> 0%
where the time goes in v1:
time: 584 us; the launch traced here: 581 us
  waiting for transfers between devices  321 us (55%)
  matrix products  82.3 us (14%)
  blocking collectives  65.2 us (11%)
  starting transfers between devices  47.6 us (8%)
  other arithmetic  34.7 us (6%)
  between operations  19.6 us (3%)
  local copies, waits for them, and re-layouts  10.5 us (2%)
    ppermute x27, waiting for transfers between devices, exchange(): lax.ppermute(value, axis, [(index, index ^ flip) for index in range(size)])  306 us
    ppermute x27, starting transfers between devices, exchange(): lax.ppermute(value, axis, [(index, index ^ flip) for index in range(size)])  47.5 us
    psum x1, blocking collectives, per_device(): lax.psum((grad_gain_one, grad_bias_one, grad_out_bias, grad_gain_two, gra...  40.5 us
    psum x1, blocking collectives, per_device(): lax.psum((jnp.sum(grad_query_all.astype(f32), axis=0), jnp.sum(grad_value...  24.7 us
    dot_general x6, matrix products, transpose_times(): lax.dot_general(left, right, (((0,), (0,)), ((), ())), preferred_element_...  21.3 us
    dot_general x10, matrix products, times_transpose(): lax.dot_general(left, right, (((1,), (1,)), ((), ())), preferred_element_...  19.5 us
    dot_general x1, matrix products, per_device(): jnp.dot(ln_two_all, up_weight, preferred_element_type=f32)  16.1 us
    psum x1, waiting for transfers between devices, per_device(): lax.psum(tuple((g.astype(bf16) for g in (grad_query, grad_key, grad_value...  15.4 us
  transfers between devices with their start and end apart: 28, of which 20 were waited for; matrix products, arithmetic and copies ran while one was open for 8% of the time, Pallas kernels for 0%

profile of v1, /device:TPU:0, one launch (start us, length us, event | category | flops | bytes accessed | tf_op | source)
XLA Modules:
  0.0 581.2 jit_solution(7384457166648815820)
XLA Ops:
  13.6 4.1 collective-permute-start.1
  21.3 36.1 %collective-permute-done.1 = bf16[256,1152]{1,0:T(8,128)(2,1)S(1)} collective-permute-done((bf16[256,1152]{1,0:T(8,128)(2,1)}, bf16[256,1152]{1,0:T(8,128)(2,1)S(1)}, u32[]{:S(2)}, u32[]{:S(2)}) %collective-permute-start.1) | collective-permute-done | bytes 589856 | tf_op jit(solution)/shard_map/ppermute | solution.py:36
  68.3 11.0 %collective-permute-start.4 = (bf16[256,1152]{1,0:T(8,128)(2,1)S(1)}, bf16[256,1152]{1,0:T(8,128)(2,1)S(1)}, u32[]{:S(2)}, u32[]{:S(2)}) collective-permute-start(bf16[256,1152]{1,0:T(8,128)(2,1)S(1)} %get-tuple-element.68), channel_id=1, source_target_pairs={{0,2},{1,3},{2,0},{3,1},{4,6},{5,7},{6,4},{7,5},{8,10},{9,11},{10,... | collective-permute-start | bytes 1769480 | tf_op jit(solution)/shard_map/ppermute | solution.py:36
  89.9 29.9 %collective-permute-done.4 = bf16[256,1152]{1,0:T(8,128)(2,1)S(1)} collective-permute-done((bf16[256,1152]{1,0:T(8,128)(2,1)S(1)}, bf16[256,1152]{1,0:T(8,128)(2,1)S(1)}, u32[]{:S(2)}, u32[]{:S(2)}) %collective-permute-start.4) | collective-permute-done | bytes 589856 | tf_op jit(solution)/shard_map/ppermute | solution.py:36
  121.6 3.6 collective-permute-start.8
  126.0 13.7 %collective-permute-done.8 = bf16[256,1152]{1,0:T(8,128)(2,1)S(1)} collective-permute-done((bf16[256,1152]{1,0:T(8,128)(2,1)S(1)}, bf16[256,1152]{1,0:T(8,128)(2,1)S(1)}, u32[]{:S(2)}, u32[]{:S(2)}) %collective-permute-start.8) | collective-permute-done | bytes 589856 | tf_op jit(solution)/shard_map/ppermute | solution.py:36
  139.8 35.3 %collective-permute-done.7 = bf16[256,1152]{1,0:T(8,128)(2,1)S(1)} collective-permute-done((bf16[256,1152]{1,0:T(8,128)(2,1)S(1)}, bf16[256,1152]{1,0:T(8,128)(2,1)S(1)}, u32[]{:S(2)}, u32[]{:S(2)}) %collective-permute-start.7) | collective-permute-done | bytes 589856 | tf_op jit(solution)/shard_map/ppermute | solution.py:36
  175.1 16.1 %convolution_add_fusion = f32[1024,1076]{0,1:T(8,128)S(1)} fusion(bf16[1152,1076]{0,1:T(8,128)(2,1)S(1)} %copy-done.61, f32[1076]{0:T(1024)S(1)} %convert_element_type.311, bf16[256,1152]{1,0:T(8,128)(2,1)S(1)} %collective-permute-done.8, bf16[256,1152]{1,0:T(8,128)(2,1)S(1)} %collective-permute-done.7, bf16[256,1152]{1,0:T(8,128)(2,1)S(1)} %collective-permute-done.6, ...), kind=kOutput, calls=%fused_computation.5 | convolution fusion | flops 2549141504 | bytes 9250000 | tf_op jit(solution)/shard_map/dot_general | solution.py:154
  191.3 5.4 fusion.118
  199.1 3.2 collective-permute-start.10
  213.3 2.9 collective-permute-done.9
  216.2 14.2 %collective-permute-done.11 = bf16[256,1152]{1,0:T(8,128)(2,1)} collective-permute-done((bf16[256,1152]{1,0:T(8,128)(2,1)}, bf16[256,1152]{1,0:T(8,128)(2,1)}, u32[]{:S(2)}, u32[]{:S(2)}) %collective-permute-start.11) | collective-permute-done | bytes 589856 | tf_op jit(solution)/shard_map/ppermute | solution.py:36
  230.4 18.3 %collective-permute-done.10 = bf16[256,1152]{1,0:T(8,128)(2,1)} collective-permute-done((bf16[256,1152]{1,0:T(8,128)(2,1)}, bf16[256,1152]{1,0:T(8,128)(2,1)}, u32[]{:S(2)}, u32[]{:S(2)}) %collective-permute-start.10) | collective-permute-done | bytes 589856 | tf_op jit(solution)/shard_map/ppermute | solution.py:36
  248.7 3.0 multiply_convert_fusion.3
  256.2 13.7 %collective-permute-done.17 = bf16[256,1152]{1,0:T(8,128)(2,1)S(1)} collective-permute-done((bf16[256,1152]{1,0:T(8,128)(2,1)S(1)}, bf16[256,1152]{1,0:T(8,128)(2,1)S(1)}, u32[]{:S(2)}, u32[]{:S(2)}) %collective-permute-start.17) | collective-permute-done | bytes 589856 | tf_op jit(solution)/shard_map/ppermute | solution.py:36
  269.8 32.5 %collective-permute-done.16 = bf16[256,1152]{1,0:T(8,128)(2,1)S(1)} collective-permute-done((bf16[256,1152]{1,0:T(8,128)(2,1)S(1)}, bf16[256,1152]{1,0:T(8,128)(2,1)S(1)}, u32[]{:S(2)}, u32[]{:S(2)}) %collective-permute-start.16) | collective-permute-done | bytes 589856 | tf_op jit(solution)/shard_map/ppermute | solution.py:36
  302.3 8.2 %convert_reduce_fusion = (f32[1076]{0:T(1024)S(1)}, bf16[1024,1076]{0,1:T(8,128)(2,1)S(1)}) fusion(f32[1024,1076]{0,1:T(8,128)S(1)} %copy-done.72, bf16[1076,1152]{1,0:T(8,128)(2,1)S(1)} %copy-done, bf16[256,1152]{1,0:T(8,128)(2,1)S(1)} %collective-permute-done.17, bf16[256,1152]{1,0:T(8,128)(2,1)S(1)} %collective-permute-done.16, ...), kind=kOutput, calls=%fused_computation.13 | convolution fusion | flops 2572278784 | bytes 11453648 | tf_op jit(solution)/shard_map/dot_general | solution.py:23
  310.6 3.6 fusion.119
  318.8 5.4 convolution_convert_fusion
  324.2 8.3 %collective-permute-done.18 = bf16[256,1152]{1,0:T(8,128)(2,1)S(1)} collective-permute-done((bf16[256,1152]{1,0:T(8,128)(2,1)S(1)}, bf16[256,1152]{1,0:T(8,128)(2,1)S(1)}, u32[]{:S(2)}, u32[]{:S(2)}) %collective-permute-start.18) | collective-permute-done | bytes 589856 | tf_op jit(solution)/shard_map/ppermute | solution.py:36
  332.4 12.2 %collective-permute-done.20 = bf16[256,1152]{1,0:T(8,128)(2,1)S(1)} collective-permute-done((bf16[256,1152]{1,0:T(8,128)(2,1)S(1)}, bf16[256,1152]{1,0:T(8,128)(2,1)S(1)}, u32[]{:S(2)}, u32[]{:S(2)}) %collective-permute-start.20) | collective-permute-done | bytes 589856 | tf_op jit(solution)/shard_map/ppermute | solution.py:36
  344.6 19.1 %collective-permute-done.19 = bf16[256,1152]{1,0:T(8,128)(2,1)S(1)} collective-permute-done((bf16[256,1152]{1,0:T(8,128)(2,1)S(1)}, bf16[256,1152]{1,0:T(8,128)(2,1)S(1)}, u32[]{:S(2)}, u32[]{:S(2)}) %collective-permute-start.19) | collective-permute-done | bytes 589856 | tf_op jit(solution)/shard_map/ppermute | solution.py:36
  367.7 4.5 fusion
  375.7 12.8 %collective-permute-done.21 = bf16[256,1152]{1,0:T(8,128)(2,1)S(1)} collective-permute-done((bf16[256,1152]{1,0:T(8,128)(2,1)S(1)}, bf16[256,1152]{1,0:T(8,128)(2,1)S(1)}, u32[]{:S(2)}, u32[]{:S(2)}) %collective-permute-start.21) | collective-permute-done | bytes 589856 | tf_op jit(solution)/shard_map/ppermute | solution.py:36
  396.4 27.1 %collective-permute-done.22 = bf16[256,1152]{1,0:T(8,128)(2,1)S(1)} collective-permute-done((bf16[256,1152]{1,0:T(8,128)(2,1)S(1)}, bf16[256,1152]{1,0:T(8,128)(2,1)S(1)}, u32[]{:S(2)}, u32[]{:S(2)}) %collective-permute-start.22) | collective-permute-done | bytes 589856 | tf_op jit(solution)/shard_map/ppermute | solution.py:36
  432.5 3.2 fusion.13
  435.7 3.2 fusion.14
  438.9 3.2 fusion.15
  453.8 24.7 %all-reduce.1 = (f32[288]{0:T(512)}, f32[288]{0:T(512)}, f32[1076]{0:T(1024)}) all-reduce(f32[288]{0:T(512)S(1)} %convert_reduce_fusion.3, f32[288]{0:T(512)S(1)} %convert_reduce_fusion.2, f32[1076]{0:T(1024)S(1)} %get-tuple-element.83), channel_id=1, replica_groups=mesh['dp'=8,'tensor'=4] {'dp'}, use_global_device_ids=true, to_apply=%region_25.26 | all-reduce | flops 1652 | bytes 13216 | tf_op jit(solution)/shard_map/psum | solution.py:230
  479.3 21.7 %collective-permute-done.25 = bf16[256,1152]{1,0:T(8,128)(2,1)} collective-permute-done((bf16[256,1152]{1,0:T(8,128)(2,1)S(1)}, bf16[256,1152]{1,0:T(8,128)(2,1)}, u32[]{:S(2)}, u32[]{:S(2)}) %collective-permute-start.25) | collective-permute-done | bytes 589856 | tf_op jit(solution)/shard_map/ppermute | solution.py:36
  504.0 40.5 %all-reduce = (f32[]{:T(128)}, f32[1152]{0:T(1024)}, f32[1152]{0:T(1024)}, f32[1152]{0:T(1024)}, f32[1152]{0:T(1024)}, /*index=5*/f32[1152]{0:T(1024)}, f32[1152]{0:T(1024)}) all-reduce(f32[]{:T(128)} %get-tuple-element.62, f32[1152]{0:T(1024)S(1)} %get-tuple-element.20, ...), channel_id=1, replica_groups=mesh['dp'=8,'tensor'=4] {'dp','tensor'}, use_global_device_ids=true, to_apply=%region_11.12 | all-reduce | flops 6913 | bytes 55304 | tf_op jit(solution)/shard_map/psum | solution.py:238
  546.5 15.4 %all-reduce.5.cloned.1.call-done = (bf16[1152,288]{0,1:T(8,128)(2,1)}, bf16[1152,288]{0,1:T(8,128)(2,1)}, bf16[1152,288]{0,1:T(8,128)(2,1)}, bf16[288,1152]{1,0:...) async-done(((bf16[1152,288]{0,1:T(8,128)(2,1)}, bf16[1152,288]{0,1:T(8,128)(2,1)}, bf16[1152,288]{0,1:T(8,128)(2,1)}, bf16[288,1152]{1,0:T(8,128)(2,1)}, ...) | async-done | bytes 7612432 | tf_op jit(solution)/shard_map/psum | solution.py:225
  (268 shorter events, 105.4 us)
Async XLA Ops:
  7.2 184.1 %copy-start = (bf16[1076,1152]{1,0:T(8,128)(2,1)S(1)}, bf16[1076,1152]{1,0:T(8,128)(2,1)}, u32[]{:S(2)}) copy-start(bf16[1076,1152]{1,0:T(8,128)(2,1)} %param.34) | copy-start | bytes 7437316
  7.2 554.7 %all-reduce.5.cloned.1.call-start = ((), (), s32[]{:S(2)}) async-start(), calls=%async_computation | async-start | bytes 15261696 | tf_op jit(solution)/shard_map/psum | solution.py:225
  13.6 43.8 %collective-permute-start.1 = (bf16[256,1152]{1,0:T(8,128)(2,1)}, bf16[256,1152]{1,0:T(8,128)(2,1)S(1)}, u32[]{:S(2)}, u32[]{:S(2)}) collective-permute-start(bf16[256,1152]{1,0:T(8,128)(2,1)} %fusion.54), channel_id=1, source_target_pairs={{0,2},{1,3},{2,0},{3,1},{4,6},{5,7},{6,4},{7,5},{8,10},{9,11},{10,... | collective-permute-start | bytes 1769480 | tf_op jit(solution)/shard_map/ppermute | solution.py:36
  17.7 39.8 %collective-permute-start.2 = (bf16[256,1152]{1,0:T(8,128)(2,1)}, bf16[256,1152]{1,0:T(8,128)(2,1)}, u32[]{:S(2)}, u32[]{:S(2)}) collective-permute-start(bf16[256,1152]{1,0:T(8,128)(2,1)} %fusion.54), channel_id=1, source_target_pairs={{0,3},{1,2},{2,1},{3,0},{4,7},{5,6},{6,5},{7,4},{8,11},{9,10},{10,... | collective-permute-start | bytes 1769480 | tf_op jit(solution)/shard_map/ppermute | solution.py:36
  19.0 60.3 %collective-permute-start = (bf16[256,1152]{1,0:T(8,128)(2,1)}, bf16[256,1152]{1,0:T(8,128)(2,1)}, u32[]{:S(2)}, u32[]{:S(2)}) collective-permute-start(bf16[256,1152]{1,0:T(8,128)(2,1)} %fusion.54), channel_id=1, source_target_pairs={{0,1},{1,0},{2,3},{3,2},{4,5},{5,4},{6,7},{7,6},{8,9},{9,8},{10,11... | collective-permute-start | bytes 1769480 | tf_op jit(solution)/shard_map/ppermute | solution.py:36
  65.4 24.4 %collective-permute-start.3 = (bf16[256,1152]{1,0:T(8,128)(2,1)S(1)}, bf16[256,1152]{1,0:T(8,128)(2,1)S(1)}, u32[]{:S(2)}, u32[]{:S(2)}) collective-permute-start(bf16[256,1152]{1,0:T(8,128)(2,1)S(1)} %get-tuple-element.67), channel_id=1, source_target_pairs={{0,3},{1,2},{2,1},{3,0},{4,7},{5,6},{6,5},{7,4},{8,11},{9,10},{10,... | collective-permute-start | bytes 1769480 | tf_op jit(solution)/shard_map/ppermute | solution.py:36
  68.3 51.4 %collective-permute-start.4 = (bf16[256,1152]{1,0:T(8,128)(2,1)S(1)}, bf16[256,1152]{1,0:T(8,128)(2,1)S(1)}, u32[]{:S(2)}, u32[]{:S(2)}) collective-permute-start(bf16[256,1152]{1,0:T(8,128)(2,1)S(1)} %get-tuple-element.68), channel_id=1, source_target_pairs={{0,2},{1,3},{2,0},{3,1},{4,6},{5,7},{6,4},{7,5},{8,10},{9,11},{10,... | collective-permute-start | bytes 1769480 | tf_op jit(solution)/shard_map/ppermute | solution.py:36
  89.3 30.5 %collective-permute-start.5 = (bf16[256,1152]{1,0:T(8,128)(2,1)S(1)}, bf16[256,1152]{1,0:T(8,128)(2,1)S(1)}, u32[]{:S(2)}, u32[]{:S(2)}) collective-permute-start(bf16[256,1152]{1,0:T(8,128)(2,1)S(1)} %slice.126), channel_id=1, source_target_pairs={{0,1},{1,0},{2,3},{3,2},{4,5},{5,4},{6,7},{7,6},{8,9},{9,8},{10,11... | collective-permute-start | bytes 1769480 | tf_op jit(solution)/shard_map/ppermute | solution.py:36
  120.3 54.8 %copy-start.61 = (bf16[1152,1076]{0,1:T(8,128)(2,1)S(1)}, bf16[1152,1076]{0,1:T(8,128)(2,1)}, u32[]{:S(2)}) copy-start(bf16[1152,1076]{0,1:T(8,128)(2,1)} %param.32) | copy-start | bytes 7437316
  121.6 18.2 %collective-permute-start.8 = (bf16[256,1152]{1,0:T(8,128)(2,1)S(1)}, bf16[256,1152]{1,0:T(8,128)(2,1)S(1)}, u32[]{:S(2)}, u32[]{:S(2)}) collective-permute-start(bf16[256,1152]{1,0:T(8,128)(2,1)S(1)} %add_convert_fusion.1), channel_id=1, source_target_pairs={{0,3},{1,2},{2,1},{3,0},{4,7},{5,6},{6,5},{7,4},{8,11},{9,10},{10,... | collective-permute-start | bytes 1769480 | tf_op jit(solution)/shard_map/ppermute | solution.py:36
  125.2 49.9 %collective-permute-start.7 = (bf16[256,1152]{1,0:T(8,128)(2,1)S(1)}, bf16[256,1152]{1,0:T(8,128)(2,1)S(1)}, u32[]{:S(2)}, u32[]{:S(2)}) collective-permute-start(bf16[256,1152]{1,0:T(8,128)(2,1)S(1)} %add_convert_fusion.1), channel_id=1, source_target_pairs={{0,2},{1,3},{2,0},{3,1},{4,6},{5,7},{6,4},{7,5},{8,10},{9,11},{10,... | collective-permute-start | bytes 1769480 | tf_op jit(solution)/shard_map/ppermute | solution.py:36
  125.2 49.9 %collective-permute-start.6 = (bf16[256,1152]{1,0:T(8,128)(2,1)S(1)}, bf16[256,1152]{1,0:T(8,128)(2,1)S(1)}, u32[]{:S(2)}, u32[]{:S(2)}) collective-permute-start(bf16[256,1152]{1,0:T(8,128)(2,1)S(1)} %add_convert_fusion.1), channel_id=1, source_target_pairs={{0,1},{1,0},{2,3},{3,2},{4,5},{5,4},{6,7},{7,6},{8,9},{9,8},{10,11... | collective-permute-start | bytes 1769480 | tf_op jit(solution)/shard_map/ppermute | solution.py:36
  197.9 18.3 %collective-permute-start.9 = (bf16[256,1152]{1,0:T(8,128)(2,1)}, bf16[256,1152]{1,0:T(8,128)(2,1)}, u32[]{:S(2)}, u32[]{:S(2)}) collective-permute-start(bf16[256,1152]{1,0:T(8,128)(2,1)} %get-tuple-element.59), channel_id=1, source_target_pairs={{0,3},{1,2},{2,1},{3,0},{4,7},{5,6},{6,5},{7,4},{8,11},{9,10},{10,... | collective-permute-start | bytes 1769480 | tf_op jit(solution)/shard_map/ppermute | solution.py:36
  199.1 31.3 %collective-permute-start.11 = (bf16[256,1152]{1,0:T(8,128)(2,1)}, bf16[256,1152]{1,0:T(8,128)(2,1)}, u32[]{:S(2)}, u32[]{:S(2)}) collective-permute-start(bf16[256,1152]{1,0:T(8,128)(2,1)} %get-tuple-element.60), channel_id=1, source_target_pairs={{0,1},{1,0},{2,3},{3,2},{4,5},{5,4},{6,7},{7,6},{8,9},{9,8},{10,11... | collective-permute-start | bytes 1769480 | tf_op jit(solution)/shard_map/ppermute | solution.py:36
  199.1 49.6 %collective-permute-start.10 = (bf16[256,1152]{1,0:T(8,128)(2,1)}, bf16[256,1152]{1,0:T(8,128)(2,1)}, u32[]{:S(2)}, u32[]{:S(2)}) collective-permute-start(bf16[256,1152]{1,0:T(8,128)(2,1)} %get-tuple-element.61), channel_id=1, source_target_pairs={{0,2},{1,3},{2,0},{3,1},{4,6},{5,7},{6,4},{7,5},{8,10},{9,11},{10,... | collective-permute-start | bytes 1769480 | tf_op jit(solution)/shard_map/ppermute | solution.py:36
  202.3 1.3 collective-permute-start.12
  204.8 3.6 collective-permute-start.13
  209.0 3.6 collective-permute-start.14
  251.7 18.2 %collective-permute-start.17 = (bf16[256,1152]{1,0:T(8,128)(2,1)S(1)}, bf16[256,1152]{1,0:T(8,128)(2,1)S(1)}, u32[]{:S(2)}, u32[]{:S(2)}) collective-permute-start(bf16[256,1152]{1,0:T(8,128)(2,1)S(1)} %get-tuple-element.52), channel_id=1, source_target_pairs={{0,3},{1,2},{2,1},{3,0},{4,7},{5,6},{6,5},{7,4},{8,11},{9,10},{10,... | collective-permute-start | bytes 1769480 | tf_op jit(solution)/shard_map/ppermute | solution.py:36
  254.1 48.2 %collective-permute-start.16 = (bf16[256,1152]{1,0:T(8,128)(2,1)S(1)}, bf16[256,1152]{1,0:T(8,128)(2,1)S(1)}, u32[]{:S(2)}, u32[]{:S(2)}) collective-permute-start(bf16[256,1152]{1,0:T(8,128)(2,1)S(1)} %get-tuple-element.52), channel_id=1, source_target_pairs={{0,2},{1,3},{2,0},{3,1},{4,6},{5,7},{6,4},{7,5},{8,10},{9,11},{10,... | collective-permute-start | bytes 1769480 | tf_op jit(solution)/shard_map/ppermute | solution.py:36
  254.1 48.2 %collective-permute-start.15 = (bf16[256,1152]{1,0:T(8,128)(2,1)S(1)}, bf16[256,1152]{1,0:T(8,128)(2,1)S(1)}, u32[]{:S(2)}, u32[]{:S(2)}) collective-permute-start(bf16[256,1152]{1,0:T(8,128)(2,1)S(1)} %get-tuple-element.52), channel_id=1, source_target_pairs={{0,1},{1,0},{2,3},{3,2},{4,5},{5,4},{6,7},{7,6},{8,9},{9,8},{10,11... | collective-permute-start | bytes 1769480 | tf_op jit(solution)/shard_map/ppermute | solution.py:36
  256.2 54.4 %copy-start.62 = (bf16[1152,1076]{0,1:T(8,128)(2,1)S(1)}, bf16[1152,1076]{0,1:T(8,128)(2,1)}, u32[]{:S(2)}) copy-start(bf16[1152,1076]{0,1:T(8,128)(2,1)} %param.32) | copy-start | bytes 7437316
  314.4 18.1 %collective-permute-start.18 = (bf16[256,1152]{1,0:T(8,128)(2,1)S(1)}, bf16[256,1152]{1,0:T(8,128)(2,1)S(1)}, u32[]{:S(2)}, u32[]{:S(2)}) collective-permute-start(bf16[256,1152]{1,0:T(8,128)(2,1)S(1)} %get-tuple-element.56), channel_id=1, source_target_pairs={{0,3},{1,2},{2,1},{3,0},{4,7},{5,6},{6,5},{7,4},{8,11},{9,10},{10,... | collective-permute-start | bytes 1769480 | tf_op jit(solution)/shard_map/ppermute | solution.py:36
  316.1 28.5 %collective-permute-start.20 = (bf16[256,1152]{1,0:T(8,128)(2,1)S(1)}, bf16[256,1152]{1,0:T(8,128)(2,1)S(1)}, u32[]{:S(2)}, u32[]{:S(2)}) collective-permute-start(bf16[256,1152]{1,0:T(8,128)(2,1)S(1)} %get-tuple-element.57), channel_id=1, source_target_pairs={{0,1},{1,0},{2,3},{3,2},{4,5},{5,4},{6,7},{7,6},{8,9},{9,8},{10,11... | collective-permute-start | bytes 1769480 | tf_op jit(solution)/shard_map/ppermute | solution.py:36
  316.1 47.6 %collective-permute-start.19 = (bf16[256,1152]{1,0:T(8,128)(2,1)S(1)}, bf16[256,1152]{1,0:T(8,128)(2,1)S(1)}, u32[]{:S(2)}, u32[]{:S(2)}) collective-permute-start(bf16[256,1152]{1,0:T(8,128)(2,1)S(1)} %get-tuple-element.58), channel_id=1, source_target_pairs={{0,2},{1,3},{2,0},{3,1},{4,6},{5,7},{6,4},{7,5},{8,10},{9,11},{10,... | collective-permute-start | bytes 1769480 | tf_op jit(solution)/shard_map/ppermute | solution.py:36
  367.6 20.9 %collective-permute-start.21 = (bf16[256,1152]{1,0:T(8,128)(2,1)S(1)}, bf16[256,1152]{1,0:T(8,128)(2,1)S(1)}, u32[]{:S(2)}, u32[]{:S(2)}) collective-permute-start(bf16[256,1152]{1,0:T(8,128)(2,1)S(1)} %convert_element_type.326), channel_id=1, source_target_pairs={{0,1},{1,0},{2,3},{3,2},{4,5},{5,4},{6,7},{7,6},{8,9},{9,8},{10,11... | collective-permute-start | bytes 1769480 | tf_op jit(solution)/shard_map/ppermute | solution.py:36
  372.3 24.2 %collective-permute-start.23 = (bf16[256,1152]{1,0:T(8,128)(2,1)S(1)}, bf16[256,1152]{1,0:T(8,128)(2,1)S(1)}, u32[]{:S(2)}, u32[]{:S(2)}) collective-permute-start(bf16[256,1152]{1,0:T(8,128)(2,1)S(1)} %convert_element_type.326), channel_id=1, source_target_pairs={{0,3},{1,2},{2,1},{3,0},{4,7},{5,6},{6,5},{7,4},{8,11},{9,10},{10,... | collective-permute-start | bytes 1769480 | tf_op jit(solution)/shard_map/ppermute | solution.py:36
  374.1 49.4 %collective-permute-start.22 = (bf16[256,1152]{1,0:T(8,128)(2,1)S(1)}, bf16[256,1152]{1,0:T(8,128)(2,1)S(1)}, u32[]{:S(2)}, u32[]{:S(2)}) collective-permute-start(bf16[256,1152]{1,0:T(8,128)(2,1)S(1)} %convert_element_type.326), channel_id=1, source_target_pairs={{0,2},{1,3},{2,0},{3,1},{4,6},{5,7},{6,4},{7,5},{8,10},{9,11},{10,... | collective-permute-start | bytes 1769480 | tf_op jit(solution)/shard_map/ppermute | solution.py:36
  445.9 32.6 %collective-permute-start.26 = (bf16[256,1152]{1,0:T(8,128)(2,1)}, bf16[256,1152]{1,0:T(8,128)(2,1)}, u32[]{:S(2)}, u32[]{:S(2)}) collective-permute-start(bf16[256,1152]{1,0:T(8,128)(2,1)} %slice.125), channel_id=1, source_target_pairs={{0,1},{1,0},{2,3},{3,2},{4,5},{5,4},{6,7},{7,6},{8,9},{9,8},{10,11... | collective-permute-start | bytes 1769480 | tf_op jit(solution)/shard_map/ppermute | solution.py:36
  450.0 28.5 %collective-permute-start.24 = (bf16[256,1152]{1,0:T(8,128)(2,1)}, bf16[256,1152]{1,0:T(8,128)(2,1)S(1)}, u32[]{:S(2)}, u32[]{:S(2)}) collective-permute-start(bf16[256,1152]{1,0:T(8,128)(2,1)} %get-tuple-element.64), channel_id=1, source_target_pairs={{0,3},{1,2},{2,1},{3,0},{4,7},{5,6},{6,5},{7,4},{8,11},{9,10},{10,... | collective-permute-start | bytes 1769480 | tf_op jit(solution)/shard_map/ppermute | solution.py:36
  451.4 49.6 %collective-permute-start.25 = (bf16[256,1152]{1,0:T(8,128)(2,1)S(1)}, bf16[256,1152]{1,0:T(8,128)(2,1)}, u32[]{:S(2)}, u32[]{:S(2)}) collective-permute-start(bf16[256,1152]{1,0:T(8,128)(2,1)S(1)} %get-tuple-element.65), channel_id=1, source_target_pairs={{0,2},{1,3},{2,0},{3,1},{4,6},{5,7},{6,4},{7,5},{8,10},{9,11},{10,... | collective-permute-start | bytes 1769480 | tf_op jit(solution)/shard_map/ppermute | solution.py:36
  478.5 66.7 %copy-start.10 = (f32[256,1152]{1,0:T(8,128)S(1)}, f32[256,1152]{1,0:T(8,128)}, u32[]{:S(2)}) copy-start(f32[256,1152]{1,0:T(8,128)} %copy-done.9) | copy-start | bytes 3538948
  (69 other events, 673.5 us)
Sparse Core Ops, SparseCore 0:
  442.2 119.6 all-reduce.4

commit v2 on v1

--- a/solution.py
+++ b/solution.py
@@ -53,6 +53,123 @@
         value = value + exchange(value, axis, flip)
         flip *= 2
     return value
+
+
+class UnitPlan:
+    def __init__(self, units):
+        self.units = units
+        self.dp = lax.axis_size("dp")
+        self.tensor = lax.axis_size("tensor")
+        self.rows = -(-units // (8 * self.dp)) * 8
+        first = (self.rows + 15) // 16 * 8
+        self.colours = [(0, first), (first, self.rows - first)]
+        self.me = lax.axis_index("dp")
+        self.here = lax.axis_index("tensor")
+        bits = [1 << k for k in range(1, self.dp.bit_length() - 1)]
+        swapped = list(bits)
+        for k in range(0, len(bits) - 1, 2):
+            swapped[k], swapped[k + 1] = swapped[k + 1], swapped[k]
+        self.steps = [bits, swapped]
+
+    def order(self, colour):
+        order = [0]
+        for flip in self.steps[colour]:
+            order = order + [flip ^ seen for seen in order]
+        return order
+
+    def piece(self, padded, flip):
+        return lax.dynamic_slice_in_dim(padded, (self.me ^ flip) * self.rows, self.rows, axis=0)
+
+    def pad(self, block):
+        short = self.dp * self.rows - self.units
+        return jnp.pad(block, ((0, short),) + ((0, 0),) * (block.ndim - 1))
+
+    def index_rows(self):
+        listed = []
+        for colour, (first, count) in enumerate(self.colours):
+            for half in (0, 1):
+                order = [half ^ seen for seen in self.order(colour)]
+                listed += [(z, e, first, count) for e in order for z in range(1, self.tensor)]
+                listed += [(0, e, first, count) for e in order]
+        return listed
+
+    def regions(self):
+        start, listed = 0, []
+        for _, count in self.colours:
+            size = self.dp // 2 * self.tensor * count
+            listed.append((start, start + size, start + 2 * size))
+            start += 2 * size
+        return listed
+
+    def natural(self, vector):
+        pieces, start = {}, 0
+        for z, e, first, count in self.index_rows():
+            pieces[z, e, first] = vector[start : start + count]
+            start += count
+        table = jnp.stack(
+            [
+                jnp.concatenate([pieces[z, e, first] for first, _ in self.colours])
+                for z in range(self.tensor)
+                for e in range(self.dp)
+            ]
+        )
+        table = xor_rows(table.reshape(self.tensor, self.dp * self.rows), self.here)
+        table = table.reshape(self.tensor * self.dp, self.rows)
+        table = xor_rows(table, self.me)
+        return table.reshape(self.tensor, self.dp * self.rows)[:, : self.units]
+
+    def arrange(self, table):
+        table = xor_rows(table.reshape(self.tensor * self.dp, self.rows), self.me)
+        table = table.reshape(self.tensor, self.dp, self.rows)
+        return jnp.concatenate(
+            [table[z, e, first : first + count] for z, e, first, count in self.index_rows()]
+        )
+
+
+def xor_rows(table, amount):
+    rows = jnp.arange(table.shape[0], dtype=jnp.int32)
+    picks = (rows[:, None] ^ amount) == rows[None, :]
+    return jnp.dot(picks.astype(jnp.float32), table, precision=lax.Precision.HIGHEST)
+
+
+def gather_units(plan, block, after):
+    padded = plan.pad(block)
+    mine, _ = lax.optimization_barrier((plan.piece(padded, 0), after))
+    foreign = [exchange(mine, "tensor", flip) for flip in range(1, plan.tensor)]
+    regions = []
+    for colour, (first, count) in enumerate(plan.colours):
+        base = jnp.concatenate([part[first : first + count] for part in foreign], axis=0)
+        for flip in plan.steps[colour]:
+            base = jnp.concatenate([base, exchange(base, "dp", flip)], axis=0)
+        for half, held in ((0, base), (1, exchange(base, "dp", 1))):
+            regions.append(held)
+            for seen in plan.order(colour):
+                own = plan.piece(padded, half ^ seen)
+                regions.append(own[first : first + count])
+    return jnp.concatenate(regions, axis=0)
+
+
+def reduce_units(plan, left, right):
+    f32, bf16 = jnp.float32, jnp.bfloat16
+    owned = []
+    for (start, middle, end), (first, count), steps in zip(
+        plan.regions(), plan.colours, plan.steps
+    ):
+        message = jnp.dot(left[middle:end], right, preferred_element_type=f32).astype(bf16)
+        total = jnp.dot(left[start:middle], right, preferred_element_type=f32)
+        total = total + exchange(message, "dp", 1).astype(f32)
+        blocks = plan.dp // 2
+        for flip in reversed(steps):
+            blocks //= 2
+            near = blocks * (plan.tensor - 1) * count
+            own = 2 * near
+            low = [total[:near], total[own : own + blocks * count]]
+            high = [total[near:own], total[own + blocks * count :]]
+            message = jnp.concatenate(high, axis=0).astype(bf16)
+            total = jnp.concatenate(low, axis=0) + exchange(message, "dp", flip).astype(f32)
+        owned.append([total[k * count : (k + 1) * count] for k in range(plan.tensor)])
+    parts = [jnp.concatenate([colour[k] for colour in owned], axis=0) for k in range(plan.tensor)]
+    return scatter_sum([parts[-1]] + parts[:-1], "tensor")
 
 
 def split_heads(block):
@@ -116,6 +233,12 @@
     states_f = states_in.astype(f32)
     ln_one, norm_one_back = jax.vjp(layer_norm, states_f, gain_one, bias_one)
     ln_one_parts = gather_parts(ln_one.astype(bf16), "tensor")
+    plan = UnitPlan(up_weight.shape[1])
+    last_part = ln_one_parts[-1]
+    bias_parts = gather_parts(plan.pad(up_bias.astype(f32)).reshape(1, -1), "tensor")
+    bias_full = plan.arrange(jnp.concatenate(bias_parts, axis=0))
+    up_full = gather_units(plan, up_weight.T, last_part)
+    down_full = gather_units(plan, down_weight, last_part)
     ln_one_img = [
         jnp.concatenate(ln_one_parts[i * share : (i + 1) * share], axis=0)
         for i in range(image_count)
@@ -150,31 +273,28 @@
     attn_out = scatter_sum(attn_parts, "tensor")
     hidden_one = states_f + attn_out + output_bias.astype(f32)
     ln_two, norm_two_back = jax.vjp(layer_norm, hidden_one, gain_two, bias_two)
-    ln_two_all = jnp.concatenate(gather_parts(ln_two.astype(bf16), "tensor"), axis=0)
-    pre_act = jnp.dot(ln_two_all, up_weight, preferred_element_type=f32) + up_bias.astype(f32)
+    ln_two_low = ln_two.astype(bf16)
+    pre_act = times_transpose(up_full, ln_two_low) + bias_full[:, None]
     activ_f, gelu_back = jax.vjp(gelu_tanh, pre_act)
     activ = activ_f.astype(bf16)
-    mlp_partial = jnp.dot(activ, down_weight, preferred_element_type=f32)
-    mlp_out = scatter_sum(
-        [mlp_partial[s * rows : (s + 1) * rows] for s in range(tensor_size)], "tensor"
-    )
+    mlp_out = transpose_times(activ, down_full)
     hidden_two = hidden_one + mlp_out + down_bias.astype(f32)
     out_states = hidden_two.astype(bf16)
     error_rows = (hidden_two - teacher.astype(f32)) * row_valid[:, None]
     squares_here = jnp.sum(error_rows * error_rows)
     grad_two = error_rows * (2.0 / token_total)
-    cot_two = jnp.concatenate(gather_parts(grad_two.astype(bf16), "tensor"), axis=0)
-    grad_down = transpose_times(activ, cot_two)
+    cot_two = grad_two.astype(bf16)
+    grad_down_own = reduce_units(plan, activ, cot_two)
     grad_down_bias = jnp.sum(grad_two, axis=0)
-    grad_activ = times_transpose(cot_two, down_weight)
+    grad_activ = times_transpose(down_full, cot_two)
     grad_pre = gelu_back(grad_activ)[0].astype(bf16)
-    grad_up = transpose_times(grad_pre, ln_two_all)
-    grad_up_bias = jnp.sum(grad_pre.astype(f32), axis=0)
-    gln_partial = times_transpose(grad_pre, up_weight)
-    grad_ln_two = scatter_sum(
-        [gln_partial[s * rows : (s + 1) * rows] for s in range(tensor_size)], "tensor"
-    )
-    mlp_grads = lax.psum((grad_down.astype(bf16), grad_up.astype(bf16)), "dp")
+    grad_up_own = reduce_units(plan, grad_pre, ln_two_low)
+    grad_up_bias_all = plan.natural(jnp.sum(grad_pre.astype(f32), axis=1))
+    grad_ln_two = transpose_times(grad_pre, up_full)
+    mlp_grads = [
+        lax.all_gather(own.astype(bf16), "dp", axis=0, tiled=True)[: plan.units]
+        for own in (grad_down_own, grad_up_own)
+    ]
     grad_hidden, grad_gain_two, grad_bias_two = norm_two_back(grad_ln_two)
     grad_one = grad_two + grad_hidden
     cot_parts = gather_parts(grad_one.astype(bf16), "tensor")
@@ -231,7 +351,6 @@
         (
             jnp.sum(grad_query_all.astype(f32), axis=0),
             jnp.sum(grad_value_all.astype(f32), axis=0),
-            grad_up_bias,
         ),
         "dp",
     )
@@ -244,6 +363,7 @@
             grad_bias_two,
             grad_down_bias,
             squares_here,
+            grad_up_bias_all,
         ),
         ("dp", "tensor"),
     )
@@ -263,7 +383,7 @@
         summed[3],
         summed[4],
         mlp_grads[1].T.astype(f32),
-        by_unit[2],
+        jnp.dot((jnp.arange(tensor_size) == here).astype(f32)[None, :], summed[7], precision=lax.Precision.HIGHEST)[0],
         mlp_grads[0].astype(f32),
         summed[5],
     )

time: 584 us -> 740 us (1.27); the launches traced: 581 us -> 729 us
  starting transfers between devices: 47.6 us -> 109 us
  local copies, waits for them, and re-layouts: 10.5 us -> 62.7 us
  other arithmetic: 34.7 us -> 53.8 us
  waiting for transfers between devices: 321 us -> 338 us
  blocking collectives: 65.2 us -> 51.9 us
  matrix products: 82.3 us -> 93.8 us
    ppermute x27 -> x54, starting transfers between devices: 47.5 us -> 108 us  [exchange(): lax.ppermute(value, axis, [(index, index ^ flip) for index in range(size)])]
    unnamed x147 -> x167, local copies, waits for them, and re-layouts: 5.97 us -> 44 us
    ppermute x27 -> x54, waiting for transfers between devices: 306 us -> 338 us  [exchange(): lax.ppermute(value, axis, [(index, index ^ flip) for index in range(size)])]
    psum x1, waiting for transfers between devices: 15.4 us -> 0.01 us  [per_device(): lax.psum(tuple((g.astype(bf16) for g in (grad_query, grad_key, grad_value...]
    psum x1, blocking collectives: 24.7 us -> 12.9 us  [per_device(): lax.psum((jnp.sum(grad_query_all.astype(f32), axis=0), jnp.sum(grad_value...]
    dot_general x10, matrix products: 19.5 us -> 29.9 us  [times_transpose(): lax.dot_general(left, right, (((1,), (1,)), ((), ())), preferred_element_...]
    dot_general x2 -> x12, matrix products: 21.5 us -> 22.1 us  [the longest x4 11.1 us: reduce_units(): total = jnp.dot(left[start:middle], right, preferred_element_type=f32)]
  transfers between devices with their start and end apart: 28 -> 57, of which waited for: 20 -> 23; matrix products, arithmetic and copies ran while one was open for 8% -> 22% of each run, Pallas kernels for 0% -> 0%
where the time goes in v2:
time: 740 us; the launch traced here: 729 us
  waiting for transfers between devices  338 us (46%)
  starting transfers between devices  109 us (15%)
  matrix products  93.8 us (13%)
  local copies, waits for them, and re-layouts  62.7 us (8%)
  other arithmetic  53.8 us (7%)
  blocking collectives  51.9 us (7%)
  between operations  19.7 us (3%)
    ppermute x54, waiting for transfers between devices, exchange(): lax.ppermute(value, axis, [(index, index ^ flip) for index in range(size)])  338 us
    ppermute x54, starting transfers between devices, exchange(): lax.ppermute(value, axis, [(index, index ^ flip) for index in range(size)])  108 us
    unnamed x167, local copies, waits for them, and re-layouts  44 us
    psum x1, blocking collectives, per_device(): lax.psum((grad_gain_one, grad_bias_one, grad_out_bias, grad_gain_two, gra...  39 us
    dot_general x10, matrix products, times_transpose(): lax.dot_general(left, right, (((1,), (1,)), ((), ())), preferred_element_...  29.9 us
    dot_general x6, matrix products, transpose_times(): lax.dot_general(left, right, (((0,), (0,)), ((), ())), preferred_element_...  23.2 us
  transfers between devices with their start and end apart: 57, of which 23 were waited for; matrix products, arithmetic and copies ran while one was open for 22% of the time, Pallas kernels for 0%

profile of v2, /device:TPU:0, one launch (start us, length us, event | category | flops | bytes accessed | tf_op | source)
XLA Modules:
  0.0 729.1 jit_solution(11884401891868432355)
XLA Ops:
  8.1 5.1 collective-permute-start.17
  50.7 15.3 %collective-permute-start.7 = (bf16[136,1152]{1,0:T(8,128)(2,1)S(1)}, bf16[136,1152]{1,0:T(8,128)(2,1)S(1)}, u32[]{:S(2)}, u32[]{:S(2)}) collective-permute-start(bf16[136,1152]{1,0:T(8,128)(2,1)S(1)} %get-tuple-element.20), channel_id=1, source_target_pairs={{0,2},{1,3},{2,0},{3,1},{4,6},{5,7},{6,4},{7,5},{8,10},{9,11},{10,... | collective-permute-start | bytes 940040 | tf_op jit(solution)/shard_map/ppermute | solution.py:36
  66.1 24.1 %collective-permute-done.1 = bf16[256,1152]{1,0:T(8,128)(2,1)} collective-permute-done((bf16[256,1152]{1,0:T(8,128)(2,1)}, bf16[256,1152]{1,0:T(8,128)(2,1)}, u32[]{:S(2)}, u32[]{:S(2)}) %collective-permute-start.1) | collective-permute-done | bytes 589856 | tf_op jit(solution)/shard_map/ppermute | solution.py:36
  109.2 6.0 collective-permute-done.18
  118.5 24.1 %collective-permute-done.19 = bf16[136,1152]{1,0:T(8,128)(2,1)S(1)} collective-permute-done((bf16[136,1152]{1,0:T(8,128)(2,1)S(1)}, bf16[136,1152]{1,0:T(8,128)(2,1)S(1)}, u32[]{:S(2)}, u32[]{:S(2)}) %collective-permute-start.19) | collective-permute-done | bytes 313376 | tf_op jit(solution)/shard_map/ppermute | solution.py:36
  151.5 29.0 %collective-permute-done.4 = bf16[256,1152]{1,0:T(8,128)(2,1)S(1)} collective-permute-done((bf16[256,1152]{1,0:T(8,128)(2,1)S(1)}, bf16[256,1152]{1,0:T(8,128)(2,1)S(1)}, u32[]{:S(2)}, u32[]{:S(2)}) %collective-permute-start.4) | collective-permute-done | bytes 589856 | tf_op jit(solution)/shard_map/ppermute | solution.py:36
  185.4 20.7 %collective-permute-done.22 = bf16[432,1152]{1,0:T(8,128)(2,1)S(1)} collective-permute-done((bf16[432,1152]{1,0:T(8,128)(2,1)S(1)}, bf16[432,1152]{1,0:T(8,128)(2,1)S(1)}, u32[]{:S(2)}, u32[]{:S(2)}) %collective-permute-start.22) | collective-permute-done | bytes 995360 | tf_op jit(solution)/shard_map/ppermute | solution.py:36
  207.3 19.3 %collective-permute-done.10 = bf16[432,1152]{1,0:T(8,128)(2,1)S(1)} collective-permute-done((bf16[432,1152]{1,0:T(8,128)(2,1)S(1)}, bf16[432,1152]{1,0:T(8,128)(2,1)S(1)}, u32[]{:S(2)}, u32[]{:S(2)}) %collective-permute-start.10) | collective-permute-done | bytes 995360 | tf_op jit(solution)/shard_map/ppermute | solution.py:36
  248.6 4.6 collective-permute-done.24
  254.8 7.4 %collective-permute-done.12 = bf16[192,1152]{1,0:T(8,128)(2,1)S(1)} collective-permute-done((bf16[192,1152]{1,0:T(8,128)(2,1)S(1)}, bf16[192,1152]{1,0:T(8,128)(2,1)S(1)}, u32[]{:S(2)}, u32[]{:S(2)}) %collective-permute-start.12) | collective-permute-done | bytes 442400 | tf_op jit(solution)/shard_map/ppermute | solution.py:36
  265.9 10.0 %collective-permute-done.25 = bf16[384,1152]{1,0:T(8,128)(2,1)S(1)} collective-permute-done((bf16[384,1152]{1,0:T(8,128)(2,1)S(1)}, bf16[384,1152]{1,0:T(8,128)(2,1)S(1)}, u32[]{:S(2)}, u32[]{:S(2)}) %collective-permute-start.25) | collective-permute-done | bytes 884768 | tf_op jit(solution)/shard_map/ppermute | solution.py:36
  276.9 16.1 %collective-permute-done.13 = bf16[384,1152]{1,0:T(8,128)(2,1)S(1)} collective-permute-done((bf16[384,1152]{1,0:T(8,128)(2,1)S(1)}, bf16[384,1152]{1,0:T(8,128)(2,1)S(1)}, u32[]{:S(2)}, u32[]{:S(2)}) %collective-permute-start.13) | collective-permute-done | bytes 884768 | tf_op jit(solution)/shard_map/ppermute | solution.py:36
  308.0 11.0 %multiply_convert_fusion = (bf16[4352,256]{0,1:T(8,128)(2,1)S(1)}, f32[4352,256]{0,1:T(8,128)}) fusion(f32[4352]{0:T(1024)S(1)} %concatenate.295, bf16[4352,1152]{1,0:T(8,128)(2,1)} %constant_dynamic-update-slice_fusion.12, bf16[256,1152]{1,0:T(8,128)(2,1)S(1)} %add_convert_fusion.1), kind=kOutput, calls=%fused_computation.18 | convolution fusion | flops 2578055168 | bytes 17318912 | tf_op jit(solution)/shard_map/dot_general | solution.py:23
  319.0 7.8 %multiply_convert_fusion.3 = (bf16[256,1152]{1,0:T(8,128)(2,1)S(1)}, f32[256,1152]{1,0:T(8,128)S(1)}) fusion(f32[]{:T(128)S(6)} %div.78, f32[256]{0:T(256)S(1)} %copy-done.48, bf16[256,1152]{1,0:T(8,128)(2,1)S(1)} %copy-done.29, f32[1152]{0:T(1024)S(1)} %copy-done.40, f32[256,1152]{1,0:T(8,128)S(1)} %get-tuple-element.72, ...), kind=kOutput, calls=%fused_computation.147 | convolution fusion | flops 2568978432 | bytes 15799812 | tf_op jit(solution)/shard_map/dot_general | solution.py:29
  326.8 10.9 %convert_reduce_fusion = (f32[4352]{0:T(1024)S(1)}, bf16[4352,256]{0,1:T(8,128)(2,1)S(1)}) fusion(f32[4352,256]{0,1:T(8,128)} %get-tuple-element.279, bf16[4352,1152]{1,0:T(8,128)(2,1)} %constant_dynamic-update-slice_fusion.42, bf16[256,1152]{1,0:T(8,128)(2,1)S(1)} %get-tuple-element.280), kind=kOutput, calls=%fused_computation.17 | convolution fusion | flops 2591420160 | bytes 17318912 | tf_op jit(solution)/shard_map/dot_general | solution.py:23
  361.2 23.7 %collective-permute-done.30 = bf16[256,1152]{1,0:T(8,128)(2,1)S(1)} collective-permute-done((bf16[256,1152]{1,0:T(8,128)(2,1)S(1)}, bf16[256,1152]{1,0:T(8,128)(2,1)S(1)}, u32[]{:S(2)}, u32[]{:S(2)}) %collective-permute-start.30) | collective-permute-done | bytes 589856 | tf_op jit(solution)/shard_map/ppermute | solution.py:36
  390.1 6.4 collective-permute-done.31
  442.9 22.5 %collective-permute-done.40 = bf16[512,1152]{1,0:T(8,128)(2,1)S(1)} collective-permute-done((bf16[512,1152]{1,0:T(8,128)(2,1)S(1)}, bf16[512,1152]{1,0:T(8,128)(2,1)S(1)}, u32[]{:S(2)}, u32[]{:S(2)}) %collective-permute-start.40) | collective-permute-done | bytes 1179680 | tf_op jit(solution)/shard_map/ppermute | solution.py:36
  467.1 7.2 collective-permute-done.37
  476.5 47.6 %collective-permute-done.41 = bf16[256,1152]{1,0:T(8,128)(2,1)S(1)} collective-permute-done((bf16[256,1152]{1,0:T(8,128)(2,1)S(1)}, bf16[256,1152]{1,0:T(8,128)(2,1)S(1)}, u32[]{:S(2)}, u32[]{:S(2)}) %collective-permute-start.41) | collective-permute-done | bytes 589856 | tf_op jit(solution)/shard_map/ppermute | solution.py:36
  530.6 12.8 %collective-permute-done.43 = bf16[136,1152]{1,0:T(8,128)(2,1)S(1)} collective-permute-done((bf16[136,1152]{1,0:T(8,128)(2,1)S(1)}, bf16[136,1152]{1,0:T(8,128)(2,1)S(1)}, u32[]{:S(2)}, u32[]{:S(2)}) %collective-permute-start.43) | collective-permute-done | bytes 313376 | tf_op jit(solution)/shard_map/ppermute | solution.py:36
  543.4 5.3 collective-permute-start.50
  558.1 11.8 %collective-permute-done.47 = bf16[288,1152]{1,0:T(8,128)(2,1)S(1)} collective-permute-done((bf16[288,1152]{1,0:T(8,128)(2,1)S(1)}, bf16[288,1152]{1,0:T(8,128)(2,1)S(1)}, u32[]{:S(2)}, u32[]{:S(2)}) %collective-permute-start.47) | collective-permute-done | bytes 663584 | tf_op jit(solution)/shard_map/ppermute | solution.py:36
  570.2 10.2 %collective-permute-start.52 = (bf16[136,1152]{1,0:T(8,128)(2,1)S(1)}, bf16[136,1152]{1,0:T(8,128)(2,1)S(1)}, u32[]{:S(2)}, u32[]{:S(2)}) collective-permute-start(bf16[136,1152]{1,0:T(8,128)(2,1)S(1)} %pad_maximum_fusion.29), channel_id=1, source_target_pairs={{0,2},{1,3},{2,0},{3,1},{4,6},{5,7},{6,4},{7,5},{8,10},{9,11},{10,... | collective-permute-start | bytes 940040 | tf_op jit(solution)/shard_map/ppermute | solution.py:36
  583.0 12.2 %collective-permute-done.52 = bf16[136,1152]{1,0:T(8,128)(2,1)S(1)} collective-permute-done((bf16[136,1152]{1,0:T(8,128)(2,1)S(1)}, bf16[136,1152]{1,0:T(8,128)(2,1)S(1)}, u32[]{:S(2)}, u32[]{:S(2)}) %collective-permute-start.52) | collective-permute-done | bytes 313376 | tf_op jit(solution)/shard_map/ppermute | solution.py:36
  595.2 6.0 collective-permute-done.53
  605.6 17.7 %collective-permute-start.34 = (bf16[256,1152]{1,0:T(8,128)(2,1)}, bf16[256,1152]{1,0:T(8,128)(2,1)}, u32[]{:S(2)}, u32[]{:S(2)}) collective-permute-start(bf16[256,1152]{1,0:T(8,128)(2,1)} %get-tuple-element.76), channel_id=1, source_target_pairs={{0,2},{1,3},{2,0},{3,1},{4,6},{5,7},{6,4},{7,5},{8,10},{9,11},{10,... | collective-permute-start | bytes 1769480 | tf_op jit(solution)/shard_map/ppermute | solution.py:36
  626.6 12.9 %all-reduce.4 = (f32[288]{0:T(512)}, f32[288]{0:T(512)}) all-reduce(f32[288]{0:T(512)S(1)} %convert_reduce_fusion.3, f32[288]{0:T(512)S(1)} %convert_reduce_fusion.2), channel_id=1, replica_groups=mesh['dp'=8,'tensor'=4] {'dp'}, use_global_device_ids=true, to_apply=%region_25.26 | all-reduce | flops 576 | bytes 4608 | tf_op jit(solution)/shard_map/psum | solution.py:350
  640.4 21.7 %collective-permute-done.34 = bf16[256,1152]{1,0:T(8,128)(2,1)} collective-permute-done((bf16[256,1152]{1,0:T(8,128)(2,1)}, bf16[256,1152]{1,0:T(8,128)(2,1)}, u32[]{:S(2)}, u32[]{:S(2)}) %collective-permute-start.34) | collective-permute-done | bytes 589856 | tf_op jit(solution)/shard_map/ppermute | solution.py:36
  665.1 39.0 %all-reduce.3 = (f32[]{:T(128)}, f32[1152]{0:T(1024)}, f32[1152]{0:T(1024)}, f32[1152]{0:T(1024)}, f32[1152]{0:T(1024)}, /*index=5*/f32[1152]{0:T(1024)}, f32[4,1076]{1,0:T(4,128)S(1)}, f32[1152]{0:T(1024)}) all-reduce(f32[]{:T(128)} %get-tuple-element.73, ...), channel_id=1, replica_groups=mesh['dp'=8,'tensor'=4] {'dp','tensor'}, use_global_device_ids=true, to_apply=%region_11.12 | all-reduce | flops 11217 | bytes 89736 | tf_op jit(solution)/shard_map/psum | solution.py:357
  712.6 4.4 convert_bitcast_fusion
  716.9 4.3 slice_convert_fusion
  (485 shorter events, 232.3 us)
Async XLA Ops:
  7.2 699.6 %all-reduce.8.cloned.1.call-start = ((), (), s32[]{:S(2)}) async-start(), calls=%async_computation.2 | async-start | bytes 5308416 | tf_op jit(solution)/shard_map/psum | solution.py:345
  8.1 34.0 %collective-permute-start.17 = (f32[1,1088]{1,0:T(1,128)S(1)}, f32[1,1088]{1,0:T(1,128)S(1)}, u32[]{:S(2)}, u32[]{:S(2)}) collective-permute-start(f32[1,1088]{1,0:T(1,128)S(1)} %reshape.268), channel_id=1, source_target_pairs={{0,3},{1,2},{2,1},{3,0},{4,7},{5,6},{6,5},{7,4},{8,11},{9,10},{10,... | collective-permute-start | bytes 13064 | tf_op jit(solution)/shard_map/ppermute | solution.py:36
  41.4 48.7 %collective-permute-start.1 = (bf16[256,1152]{1,0:T(8,128)(2,1)}, bf16[256,1152]{1,0:T(8,128)(2,1)}, u32[]{:S(2)}, u32[]{:S(2)}) collective-permute-start(bf16[256,1152]{1,0:T(8,128)(2,1)} %fusion.54), channel_id=1, source_target_pairs={{0,2},{1,3},{2,0},{3,1},{4,6},{5,7},{6,4},{7,5},{8,10},{9,11},{10,... | collective-permute-start | bytes 1769480 | tf_op jit(solution)/shard_map/ppermute | solution.py:36
  42.1 58.0 %collective-permute-start = (bf16[256,1152]{1,0:T(8,128)(2,1)}, bf16[256,1152]{1,0:T(8,128)(2,1)}, u32[]{:S(2)}, u32[]{:S(2)}) collective-permute-start(bf16[256,1152]{1,0:T(8,128)(2,1)} %fusion.54), channel_id=1, source_target_pairs={{0,1},{1,0},{2,3},{3,2},{4,5},{5,4},{6,7},{7,6},{8,9},{9,8},{10,11... | collective-permute-start | bytes 1769480 | tf_op jit(solution)/shard_map/ppermute | solution.py:36
  46.9 103.2 %collective-permute-start.8 = (bf16[136,1152]{1,0:T(8,128)(2,1)S(1)}, bf16[136,1152]{1,0:T(8,128)(2,1)S(1)}, u32[]{:S(2)}, u32[]{:S(2)}) collective-permute-start(bf16[136,1152]{1,0:T(8,128)(2,1)S(1)} %get-tuple-element.20), channel_id=1, source_target_pairs={{0,3},{1,2},{2,1},{3,0},{4,7},{5,6},{6,5},{7,4},{8,11},{9,10},{10,... | collective-permute-start | bytes 940040 | tf_op jit(solution)/shard_map/ppermute | solution.py:36
  50.7 96.7 %collective-permute-start.7 = (bf16[136,1152]{1,0:T(8,128)(2,1)S(1)}, bf16[136,1152]{1,0:T(8,128)(2,1)S(1)}, u32[]{:S(2)}, u32[]{:S(2)}) collective-permute-start(bf16[136,1152]{1,0:T(8,128)(2,1)S(1)} %get-tuple-element.20), channel_id=1, source_target_pairs={{0,2},{1,3},{2,0},{3,1},{4,6},{5,7},{6,4},{7,5},{8,10},{9,11},{10,... | collective-permute-start | bytes 940040 | tf_op jit(solution)/shard_map/ppermute | solution.py:36
  66.1 49.8 %collective-permute-start.6 = (bf16[136,1152]{1,0:T(8,128)(2,1)S(1)}, bf16[136,1152]{1,0:T(8,128)(2,1)S(1)}, u32[]{:S(2)}, u32[]{:S(2)}) collective-permute-start(bf16[136,1152]{1,0:T(8,128)(2,1)S(1)} %get-tuple-element.20), channel_id=1, source_target_pairs={{0,1},{1,0},{2,3},{3,2},{4,5},{5,4},{6,7},{7,6},{8,9},{9,8},{10,11... | collective-permute-start | bytes 940040 | tf_op jit(solution)/shard_map/ppermute | solution.py:36
  90.2 53.2 %collective-permute-start.20 = (bf16[136,1152]{1,0:T(8,128)(2,1)}, bf16[136,1152]{1,0:T(8,128)(2,1)S(1)}, u32[]{:S(2)}, u32[]{:S(2)}) collective-permute-start(bf16[136,1152]{1,0:T(8,128)(2,1)} %get-tuple-element.21), channel_id=1, source_target_pairs={{0,3},{1,2},{2,1},{3,0},{4,7},{5,6},{6,5},{7,4},{8,11},{9,10},{10,... | collective-permute-start | bytes 940040 | tf_op jit(solution)/shard_map/ppermute | solution.py:36
  115.9 35.6 %collective-permute-start.3 = (bf16[256,1152]{1,0:T(8,128)(2,1)S(1)}, bf16[256,1152]{1,0:T(8,128)(2,1)S(1)}, u32[]{:S(2)}, u32[]{:S(2)}) collective-permute-start(bf16[256,1152]{1,0:T(8,128)(2,1)S(1)} %get-tuple-element.78), channel_id=1, source_target_pairs={{0,3},{1,2},{2,1},{3,0},{4,7},{5,6},{6,5},{7,4},{8,11},{9,10},{10,... | collective-permute-start | bytes 1769480 | tf_op jit(solution)/shard_map/ppermute | solution.py:36
  142.6 37.9 %collective-permute-start.4 = (bf16[256,1152]{1,0:T(8,128)(2,1)S(1)}, bf16[256,1152]{1,0:T(8,128)(2,1)S(1)}, u32[]{:S(2)}, u32[]{:S(2)}) collective-permute-start(bf16[256,1152]{1,0:T(8,128)(2,1)S(1)} %get-tuple-element.79), channel_id=1, source_target_pairs={{0,2},{1,3},{2,0},{3,1},{4,6},{5,7},{6,4},{7,5},{8,10},{9,11},{10,... | collective-permute-start | bytes 1769480 | tf_op jit(solution)/shard_map/ppermute | solution.py:36
  143.3 37.2 %collective-permute-start.5 = (bf16[256,1152]{1,0:T(8,128)(2,1)S(1)}, bf16[256,1152]{1,0:T(8,128)(2,1)S(1)}, u32[]{:S(2)}, u32[]{:S(2)}) collective-permute-start(bf16[256,1152]{1,0:T(8,128)(2,1)S(1)} %slice.1331), channel_id=1, source_target_pairs={{0,1},{1,0},{2,3},{3,2},{4,5},{5,4},{6,7},{7,6},{8,9},{9,8},{10,11... | collective-permute-start | bytes 1769480 | tf_op jit(solution)/shard_map/ppermute | solution.py:36
  147.4 33.6 %collective-permute-start.21 = (bf16[216,1152]{1,0:T(8,128)(2,1)S(1)}, bf16[216,1152]{1,0:T(8,128)(2,1)S(1)}, u32[]{:S(2)}, u32[]{:S(2)}) collective-permute-start(bf16[216,1152]{1,0:T(8,128)(2,1)S(1)} %pad_maximum_fusion.17), channel_id=1, source_target_pairs={{0,8},{4,12},{8,0},{12,4},{16,24},{20,28},{24,16},{28,20},{1,9},{5... | collective-permute-start | bytes 1493000 | tf_op jit(solution)/shard_map/ppermute | solution.py:36
  150.9 31.8 %collective-permute-start.9 = (bf16[216,1152]{1,0:T(8,128)(2,1)S(1)}, bf16[216,1152]{1,0:T(8,128)(2,1)S(1)}, u32[]{:S(2)}, u32[]{:S(2)}) collective-permute-start(bf16[216,1152]{1,0:T(8,128)(2,1)S(1)} %pad_maximum_fusion.16), channel_id=1, source_target_pairs={{0,8},{4,12},{8,0},{12,4},{16,24},{20,28},{24,16},{28,20},{1,9},{5... | collective-permute-start | bytes 1493000 | tf_op jit(solution)/shard_map/ppermute | solution.py:36
  182.8 43.7 %collective-permute-start.10 = (bf16[432,1152]{1,0:T(8,128)(2,1)S(1)}, bf16[432,1152]{1,0:T(8,128)(2,1)S(1)}, u32[]{:S(2)}, u32[]{:S(2)}) collective-permute-start(bf16[432,1152]{1,0:T(8,128)(2,1)S(1)} %pad_maximum_fusion.6), channel_id=1, source_target_pairs={{0,16},{4,20},{8,24},{12,28},{16,0},{20,4},{24,8},{28,12},{1,17},{... | collective-permute-start | bytes 2985992 | tf_op jit(solution)/shard_map/ppermute | solution.py:36
  344.2 45.3 %collective-permute-start.32 = (bf16[256,1152]{1,0:T(8,128)(2,1)S(1)}, bf16[256,1152]{1,0:T(8,128)(2,1)S(1)}, u32[]{:S(2)}, u32[]{:S(2)}) collective-permute-start(bf16[256,1152]{1,0:T(8,128)(2,1)S(1)} %convert_element_type.382), channel_id=1, source_target_pairs={{0,3},{1,2},{2,1},{3,0},{4,7},{5,6},{6,5},{7,4},{8,11},{9,10},{10,... | collective-permute-start | bytes 1769480 | tf_op jit(solution)/shard_map/ppermute | solution.py:36
  346.2 50.3 %collective-permute-start.31 = (bf16[256,1152]{1,0:T(8,128)(2,1)S(1)}, bf16[256,1152]{1,0:T(8,128)(2,1)S(1)}, u32[]{:S(2)}, u32[]{:S(2)}) collective-permute-start(bf16[256,1152]{1,0:T(8,128)(2,1)S(1)} %convert_element_type.382), channel_id=1, source_target_pairs={{0,2},{1,3},{2,0},{3,1},{4,6},{5,7},{6,4},{7,5},{8,10},{9,11},{10,... | collective-permute-start | bytes 1769480 | tf_op jit(solution)/shard_map/ppermute | solution.py:36
  346.2 38.6 %collective-permute-start.30 = (bf16[256,1152]{1,0:T(8,128)(2,1)S(1)}, bf16[256,1152]{1,0:T(8,128)(2,1)S(1)}, u32[]{:S(2)}, u32[]{:S(2)}) collective-permute-start(bf16[256,1152]{1,0:T(8,128)(2,1)S(1)} %convert_element_type.382), channel_id=1, source_target_pairs={{0,1},{1,0},{2,3},{3,2},{4,5},{5,4},{6,7},{7,6},{8,9},{9,8},{10,11... | collective-permute-start | bytes 1769480 | tf_op jit(solution)/shard_map/ppermute | solution.py:36
  353.3 72.0 %collective-permute-start.48 = (bf16[1024,1152]{1,0:T(8,128)(2,1)}, bf16[1024,1152]{1,0:T(8,128)(2,1)}, u32[]{:S(2)}, u32[]{:S(2)}) collective-permute-start(bf16[1024,1152]{1,0:T(8,128)(2,1)} %convolution_convert_fusion.2), channel_id=1, source_target_pairs={{0,4},{4,0},{8,12},{12,8},{16,20},{20,16},{24,28},{28,24},{1,5},{5... | collective-permute-start | bytes 7077896 | tf_op jit(solution)/shard_map/ppermute | solution.py:36
  353.3 68.8 %collective-permute-start.39 = (bf16[1024,1152]{1,0:T(8,128)(2,1)}, bf16[1024,1152]{1,0:T(8,128)(2,1)}, u32[]{:S(2)}, u32[]{:S(2)}) collective-permute-start(bf16[1024,1152]{1,0:T(8,128)(2,1)} %convolution_convert_fusion.3), channel_id=1, source_target_pairs={{0,4},{4,0},{8,12},{12,8},{16,20},{20,16},{24,28},{28,24},{1,5},{5... | collective-permute-start | bytes 7077896 | tf_op jit(solution)/shard_map/ppermute | solution.py:36
  384.8 51.9 %collective-permute-start.45 = (bf16[1152,1152]{1,0:T(8,128)(2,1)}, bf16[1152,1152]{1,0:T(8,128)(2,1)}, u32[]{:S(2)}, u32[]{:S(2)}) collective-permute-start(bf16[1152,1152]{1,0:T(8,128)(2,1)} %convolution_convert_fusion), channel_id=1, source_target_pairs={{0,4},{4,0},{8,12},{12,8},{16,20},{20,16},{24,28},{28,24},{1,5},{5... | collective-permute-start | bytes 7962632 | tf_op jit(solution)/shard_map/ppermute | solution.py:36
  389.5 42.5 %collective-permute-start.36 = (bf16[1152,1152]{1,0:T(8,128)(2,1)}, bf16[1152,1152]{1,0:T(8,128)(2,1)}, u32[]{:S(2)}, u32[]{:S(2)}) collective-permute-start(bf16[1152,1152]{1,0:T(8,128)(2,1)} %convolution_convert_fusion.1), channel_id=1, source_target_pairs={{0,4},{4,0},{8,12},{12,8},{16,20},{20,16},{24,28},{28,24},{1,5},{5... | collective-permute-start | bytes 7962632 | tf_op jit(solution)/shard_map/ppermute | solution.py:36
  402.6 237.0 %collective-permute-start.35 = (bf16[256,1152]{1,0:T(8,128)(2,1)}, bf16[256,1152]{1,0:T(8,128)(2,1)}, u32[]{:S(2)}, u32[]{:S(2)}) collective-permute-start(bf16[256,1152]{1,0:T(8,128)(2,1)} %slice.1330), channel_id=1, source_target_pairs={{0,1},{1,0},{2,3},{3,2},{4,5},{5,4},{6,7},{7,6},{8,9},{9,8},{10,11... | collective-permute-start | bytes 1769480 | tf_op jit(solution)/shard_map/ppermute | solution.py:36
  417.6 294.9 %all-gather.3.cloned.1.call-start = ((), (), s32[]{:S(2)}) async-start(), calls=%async_computation | async-start | bytes 2820096 | tf_op jit(solution)/shard_map/all_gather | solution.py:295
  429.8 35.6 %collective-permute-start.40 = (bf16[512,1152]{1,0:T(8,128)(2,1)S(1)}, bf16[512,1152]{1,0:T(8,128)(2,1)S(1)}, u32[]{:S(2)}, u32[]{:S(2)}) collective-permute-start(bf16[512,1152]{1,0:T(8,128)(2,1)S(1)} %pad_maximum_fusion.4), channel_id=1, source_target_pairs={{0,8},{4,12},{8,0},{12,4},{16,24},{20,28},{24,16},{28,20},{1,9},{5... | collective-permute-start | bytes 3538952 | tf_op jit(solution)/shard_map/ppermute | solution.py:36
  431.5 96.9 %collective-permute-start.49 = (bf16[512,1152]{1,0:T(8,128)(2,1)S(1)}, bf16[512,1152]{1,0:T(8,128)(2,1)S(1)}, u32[]{:S(2)}, u32[]{:S(2)}) collective-permute-start(bf16[512,1152]{1,0:T(8,128)(2,1)S(1)} %pad_maximum_fusion.5), channel_id=1, source_target_pairs={{0,8},{4,12},{8,0},{12,4},{16,24},{20,28},{24,16},{28,20},{1,9},{5... | collective-permute-start | bytes 3538952 | tf_op jit(solution)/shard_map/ppermute | solution.py:36
  435.0 39.3 %collective-permute-start.37 = (bf16[576,1152]{1,0:T(8,128)(2,1)S(1)}, bf16[576,1152]{1,0:T(8,128)(2,1)S(1)}, u32[]{:S(2)}, u32[]{:S(2)}) collective-permute-start(bf16[576,1152]{1,0:T(8,128)(2,1)S(1)} %pad_maximum_fusion.1), channel_id=1, source_target_pairs={{0,16},{4,20},{8,24},{12,28},{16,0},{20,4},{24,8},{28,12},{1,17},{... | collective-permute-start | bytes 3981320 | tf_op jit(solution)/shard_map/ppermute | solution.py:36
  442.4 107.4 %collective-permute-start.46 = (bf16[576,1152]{1,0:T(8,128)(2,1)}, bf16[576,1152]{1,0:T(8,128)(2,1)}, u32[]{:S(2)}, u32[]{:S(2)}) collective-permute-start(bf16[576,1152]{1,0:T(8,128)(2,1)} %pad_maximum_fusion.2), channel_id=1, source_target_pairs={{0,16},{4,20},{8,24},{12,28},{16,0},{20,4},{24,8},{28,12},{1,17},{... | collective-permute-start | bytes 3981320 | tf_op jit(solution)/shard_map/ppermute | solution.py:36
  465.9 58.2 %collective-permute-start.41 = (bf16[256,1152]{1,0:T(8,128)(2,1)S(1)}, bf16[256,1152]{1,0:T(8,128)(2,1)S(1)}, u32[]{:S(2)}, u32[]{:S(2)}) collective-permute-start(bf16[256,1152]{1,0:T(8,128)(2,1)S(1)} %pad_maximum_fusion.14), channel_id=1, source_target_pairs={{0,16},{4,20},{8,24},{12,28},{16,0},{20,4},{24,8},{28,12},{1,17},{... | collective-permute-start | bytes 1769480 | tf_op jit(solution)/shard_map/ppermute | solution.py:36
  474.9 49.4 %collective-permute-start.38 = (bf16[288,1152]{1,0:T(8,128)(2,1)S(1)}, bf16[288,1152]{1,0:T(8,128)(2,1)S(1)}, u32[]{:S(2)}, u32[]{:S(2)}) collective-permute-start(bf16[288,1152]{1,0:T(8,128)(2,1)S(1)} %pad_maximum_fusion.10), channel_id=1, source_target_pairs={{0,8},{4,12},{8,0},{12,4},{16,24},{20,28},{24,16},{28,20},{1,9},{5... | collective-permute-start | bytes 1990664 | tf_op jit(solution)/shard_map/ppermute | solution.py:36
  549.6 167.4 %all-gather.5.cloned.1.call-start = ((), (), s32[]{:S(2)}) async-start(), calls=%async_computation.1 | async-start | bytes 2820096 | tf_op jit(solution)/shard_map/all_gather | solution.py:295
  603.3 36.3 %collective-permute-start.33 = (bf16[256,1152]{1,0:T(8,128)(2,1)}, bf16[256,1152]{1,0:T(8,128)(2,1)S(1)}, u32[]{:S(2)}, u32[]{:S(2)}) collective-permute-start(bf16[256,1152]{1,0:T(8,128)(2,1)} %get-tuple-element.75), channel_id=1, source_target_pairs={{0,3},{1,2},{2,1},{3,0},{4,7},{5,6},{6,5},{7,4},{8,11},{9,10},{10,... | collective-permute-start | bytes 1769480 | tf_op jit(solution)/shard_map/ppermute | solution.py:36
  605.6 56.5 %collective-permute-start.34 = (bf16[256,1152]{1,0:T(8,128)(2,1)}, bf16[256,1152]{1,0:T(8,128)(2,1)}, u32[]{:S(2)}, u32[]{:S(2)}) collective-permute-start(bf16[256,1152]{1,0:T(8,128)(2,1)} %get-tuple-element.76), channel_id=1, source_target_pairs={{0,2},{1,3},{2,0},{3,1},{4,6},{5,7},{6,4},{7,5},{8,10},{9,11},{10,... | collective-permute-start | bytes 1769480 | tf_op jit(solution)/shard_map/ppermute | solution.py:36
  (83 other events, 1514.1 us)
Sparse Core Ops, SparseCore 0:
  417.8 87.6 all-reduce.7
  549.7 35.0 all-gather.2
  602.3 44.7 all-gather.4
